TPU v7x, 512 devices: a whole 4x8x8 slice. The times are simulated.
512 devices in a mesh: ep: 16 (over z_hi, y), sp: 32 (over z_lo, x, core).
Axes of the slice: x: 4, y: 8, z: 8 (z_hi: 2, z_lo: 4; z = z_hi * 4 + z_lo), core: 2. Of those that a mesh axis runs over, the one named last changes fastest.
Arguments:
- grad_out: bfloat16 [65536, 4096], P(('ep', 'sp')), may hold values from -1.5 to 1.5
- routes: int32 [65536, 8], P(('ep', 'sp')), may hold values from 0 to 127, as said below
- gate: bfloat16 [65536, 8], P(('ep', 'sp')), may hold values from 0.049804688 to 1
- saved: bfloat16 [16, 32, 256, 3072], P('ep', 'sp'), may hold values from -6 to 6
- w_down: bfloat16 [16, 1536, 4096], P('ep', None, 'sp'), may hold values from -0.15625 to 0.15625
Outputs:
- grad_pre: bfloat16 [16, 32, 256, 3072], P('ep', 'sp')
- grad_gate: float32 [65536, 8], P(('ep', 'sp'))
Inputs may be any that keep to these rules, and one draw needn't show every extreme that they name: `routes`: each row names 8 different experts. In every block of 128 rows at most 16 rows name the same expert whose number is a multiple of 8, and in every block one such expert is named by exactly 16 rows; it is the same expert for all blocks whose indices agree modulo 32.
All inputs are finite; a program needn't handle non-finite values.
Results may differ from a plain program's by a relative error of at most 0.0029.
Values may be sent and summed in bfloat16 or wider, within the bound.
No kernel may reach another device: no remote copies, remote signals or barrier semaphores. Data moves between devices by JAX's collectives and lax.ppermute only.
A program may use at most 128 MiB of HBM per device.

v0:
```python
import functools

import jax
import jax.numpy as jnp
from jax import lax
from jax.experimental import pallas as pl
from jax.experimental.pallas import tpu as pltpu
from jax.sharding import Mesh, PartitionSpec as P


LANES = 128
CAPACITY = 16
STEP = 8
EP = ("zh", "y")
STAY, CROSS = 3, 4
F32, BF16 = jnp.float32, jnp.bfloat16
VMEM = pl.BlockSpec(memory_space=pltpu.VMEM)
SMEM = pl.BlockSpec(memory_space=pltpu.SMEM)


def ring(size, shift):
    return [((i + shift) % size, i) for i in range(size)]


def pack_kernel(core_ref, tokens_ref, routes_ref, keep_ref, send_ref):
    core = core_ref[0]
    rows = tokens_ref.shape[0]
    for ref, parity in ((keep_ref, core), (send_ref, 1 - core)):
        for b in range(ref.shape[1] // LANES):
            start = pl.multiple_of((2 * b + parity) * LANES, LANES)
            ref[:rows, b * LANES : (b + 1) * LANES] = tokens_ref[:, pl.ds(start, LANES)]
    send_ref[rows:, :] = jnp.zeros((send_ref.shape[0] - rows, send_ref.shape[1]), BF16)
    routes = routes_ref[...].astype(F32)
    send_ref[rows:, :LANES] = jnp.concatenate([routes, routes], axis=0).astype(BF16)


def places(routes, experts, first=0):
    tokens = routes.shape[1]
    wanted = (STEP * (lax.broadcasted_iota(jnp.int32, (experts, tokens), 0) + first)).astype(F32)
    hits = [routes[k : k + 1, :] == wanted for k in range(routes.shape[0])]
    member = functools.reduce(jnp.add, [h.astype(F32) for h in hits])
    before = lax.broadcasted_iota(jnp.int32, (tokens, tokens), 0) < lax.broadcasted_iota(
        jnp.int32, (tokens, tokens), 1
    )
    place = lax.dot_general(
        member.astype(BF16),
        before.astype(F32).astype(BF16),
        (((1,), (0,)), ((), ())),
        preferred_element_type=F32,
    )
    return hits, jnp.where(member > 0.5, place, -1.0)


def one_hot(place, capacity):
    experts, tokens = place.shape
    spread = jnp.broadcast_to(place[:, None, :], (experts, capacity, tokens))
    slot = lax.broadcasted_iota(jnp.int32, (experts, capacity, tokens), 1).astype(F32)
    return (spread == slot).astype(F32).reshape(experts * capacity, tokens)


def eye(shape):
    return lax.broadcasted_iota(jnp.int32, shape, 1) == lax.broadcasted_iota(jnp.int32, shape, 2)


def to_lanes(column, sources):
    rows = column.shape[0]
    shape = (sources, rows // sources, LANES)
    spread = jnp.broadcast_to(column, (rows, LANES)).reshape(shape)
    return jnp.sum(jnp.where(eye(shape), spread, 0.0), axis=1, keepdims=True)


def to_column(line, capacity):
    sources = line.shape[0]
    shape = (sources, capacity, LANES)
    spread = jnp.where(eye(shape), jnp.broadcast_to(line, shape), 0.0)
    return jnp.sum(spread.reshape(sources * capacity, LANES), axis=1, keepdims=True)


def send_rows(place, tokens_ref, out_ref, base):
    tokens = place.shape[1]
    experts, _, lanes = out_ref.shape
    chosen = one_hot(place, CAPACITY)
    rows = jnp.dot(chosen.astype(BF16), tokens_ref[:tokens, :], preferred_element_type=F32)
    rows = rows.astype(BF16)
    for b in range(rows.shape[1] // lanes):
        start = base + b * CAPACITY
        out_ref[:, start : start + CAPACITY, :] = rows[:, b * lanes : (b + 1) * lanes].reshape(
            experts, CAPACITY, lanes
        )
    return chosen


def dispatch_kernel(side, theirs, mine, info_ref, got_ref, keep_ref, routes_ref, gate_ref, out_ref):
    experts = out_ref.shape[0]
    first = info_ref[side] * experts
    height = got_ref.shape[1] // LANES * CAPACITY
    if theirs:
        table = got_ref[LANES:, :LANES].astype(F32)
        _, place = places(table[: table.shape[0] // 2], experts, first)
        send_rows(place, got_ref, out_ref, 0)
    if mine:
        base = height if theirs else 0
        gate = gate_ref[...].astype(F32)
        hits, place = places(routes_ref[...].astype(F32), experts, first)
        chosen = send_rows(place, keep_ref, out_ref, base)
        gates = functools.reduce(
            jnp.add, [jnp.where(h, gate[k : k + 1, :], 0.0) for k, h in enumerate(hits)]
        )
        spread = jnp.broadcast_to(gates[:, None, :], (experts, CAPACITY, gates.shape[1]))
        column = jnp.sum(chosen * spread.reshape(chosen.shape), axis=1, keepdims=True)
        line = to_lanes(column, experts)
        out_ref[:, base + height :, :] = jnp.broadcast_to(line, (experts, 8, LANES)).astype(BF16)


def take_rows(shifts, info_ref, sections, rows_ref):
    slots = rows_ref.shape[0] // len(sections)
    for m, (ref, base) in enumerate(sections):
        capacity = slots // ref.shape[0]
        for n, (dz, dx) in enumerate(shifts):
            chip = ((info_ref[1] + dz) & 3) * 4 + ((info_ref[2] + dx) & 3)
            start = pl.multiple_of(base + chip * capacity, capacity)
            rows_ref[m * slots : (m + 1) * slots, n * LANES : (n + 1) * LANES] = ref[
                :, pl.ds(start, capacity), :
            ].reshape(slots, LANES)


def theirs_kernel(shifts, info_ref, stay_ref, cross_ref, *refs):
    weights, (out_ref, whole_ref, rows_ref) = refs[:-3], refs[-3:]

    @pl.when(pl.program_id(0) == 0)
    def _():
        take_rows(shifts, info_ref, ((stay_ref, 0), (cross_ref, 0)), rows_ref)

    block = jnp.concatenate([w[i] for w in weights for i in range(w.shape[0])], axis=1)
    step = block.shape[0]
    whole_ref[pl.ds(pl.multiple_of(pl.program_id(0) * step, step), step), :] = block
    out_ref[...] = lax.dot_general(
        rows_ref[...], block, (((1,), (1,)), ((), ())), preferred_element_type=F32
    )


def mine_kernel(shifts, base, info_ref, stay_ref, cross_ref, whole_ref, out_ref, rows_ref):
    @pl.when(pl.program_id(0) == 0)
    def _():
        take_rows(shifts, info_ref, ((stay_ref, base), (cross_ref, 0)), rows_ref)

    step = out_ref.shape[1]
    block = whole_ref[pl.ds(pl.multiple_of(pl.program_id(0) * step, step), step), :]
    out_ref[...] = lax.dot_general(
        rows_ref[...], block, (((1,), (1,)), ((), ())), preferred_element_type=F32
    )


def piece(i, info):
    return ((i // 2) ^ info[STAY]) * 2 + i % 2


def finish_kernel(
    info_ref, mine_ref, theirs_ref, saved_ref, stay_ref, cross_ref, out_ref, score_ref
):
    rows, units = mine_ref.shape
    number = piece(pl.program_id(0), info_ref)
    here = pl.ds(pl.multiple_of(number * rows, rows), rows)
    sources = score_ref.shape[0]
    step = 256
    total = jnp.zeros((rows, 1), F32)
    line = jnp.where(number < 2, stay_ref[...].astype(F32), cross_ref[...].astype(F32))
    gate_in = to_column(line[:, :1, :], rows // sources)
    for j in range(units // step):
        cols = slice(j * step, (j + 1) * step)
        up_cols = slice(units + j * step, units + (j + 1) * step)
        grad = mine_ref[:, cols] + theirs_ref[here, cols]
        a = saved_ref[:, cols].astype(F32)
        u = saved_ref[:, up_cols].astype(F32)
        sig = 1.0 / (1.0 + jnp.exp(-a))
        silu = a * sig
        hidden = (silu * u).astype(BF16).astype(F32)
        total += jnp.sum(grad * hidden, axis=1, keepdims=True)
        scaled = grad * gate_in
        out_ref[:, cols] = (scaled * u * sig * (1.0 + a * (1.0 - sig))).astype(BF16)
        out_ref[:, up_cols] = (scaled * silu).astype(BF16)
    score_ref[...] = jnp.broadcast_to(to_lanes(total, sources), score_ref.shape)


def home_kernel(routes_ref, back_ref, out_ref):
    experts = back_ref.shape[0]
    routes = routes_ref[...].astype(F32)
    hits, place = places(routes, experts)
    chosen = one_hot(place, CAPACITY)
    column = to_column(back_ref[:, :1, :], CAPACITY)
    score = jnp.sum((column * chosen).reshape(experts, CAPACITY, -1), axis=1)
    for k, h in enumerate(hits):
        out_ref[k : k + 1, :] = jnp.sum(jnp.where(h, score, 0.0), axis=0, keepdims=True)


def call(kernel, shapes, in_specs, out_specs, scratch=(), grid=(), prefetch=0):
    return pl.pallas_call(
        kernel,
        out_shape=shapes,
        grid_spec=pltpu.PrefetchScalarGridSpec(
            num_scalar_prefetch=prefetch,
            grid=grid,
            in_specs=in_specs,
            out_specs=out_specs,
            scratch_shapes=list(scratch),
        ),
        compiler_params=pltpu.CompilerParams(vmem_limit_bytes=24 << 20),
    )


def near(array):
    return pltpu.with_memory_space_constraint(array, pltpu.VMEM)


def far(array):
    return pltpu.with_memory_space_constraint(array, pltpu.HBM)


def permute(array, axis, shift):
    return lax.ppermute(array, axis, ring(4, shift))


def gather_weights(block):
    z1, z3, z2 = (permute(block, "zl", r) for r in (1, 3, 2))
    trio = jnp.concatenate([block, z1, z3], axis=0)
    g1, g3 = permute(trio, "x", 1), permute(trio, "x", 3)
    h1, h3 = permute(z2, "x", 1), permute(z2, "x", 3)
    f1 = permute(g1[:2], "x", 1)
    f3 = permute(g3[2:], "x", 3)
    f2 = permute(h3, "x", 3)
    groups = [(trio, (0, 1, 3), 0), (g1, (0, 1, 3), 1), (g3, (0, 1, 3), 3)]
    groups += [(z2, (2,), 0), (h1, (2,), 1), (h3, (2,), 3)]
    return groups + [(f1, (0, 1), 2), (f3, (3,), 2), (f2, (2,), 2)]


def step(grad_out, routes, gate, saved, w_down):
    tokens, width = grad_out.shape
    units, slots = w_down.shape[1], saved.shape[2]
    sources = slots // CAPACITY
    groups = gather_weights(w_down)
    info = jnp.stack(
        [lax.axis_index(a) for a in ("c", "zl", "x", "zh")] + [1 - lax.axis_index("zh")]
    ).astype(jnp.int32)
    half = width // 2
    blocks = half // LANES
    routes_t, gate_t = routes.T, gate.T
    keep, send = call(
        pack_kernel,
        (
            jax.ShapeDtypeStruct((tokens, half), BF16),
            jax.ShapeDtypeStruct((tokens + 16, half), BF16),
        ),
        [SMEM, VMEM, VMEM],
        (VMEM, VMEM),
    )(info, far(grad_out), far(routes_t))
    got = lax.ppermute(send, "c", ring(2, 1))
    height = CAPACITY * blocks
    peers = sources // 2

    def along_y(side, theirs, mine):
        rows = height * (theirs + mine) + 8 * mine
        array = call(
            functools.partial(dispatch_kernel, side, theirs, mine),
            jax.ShapeDtypeStruct((peers, rows, LANES), BF16),
            [SMEM] + [VMEM] * 4,
            VMEM,
        )(info, got, keep, far(routes_t), far(gate_t))
        return lax.all_to_all(array, "y", split_axis=0, concat_axis=0, tiled=True)

    def across(array):
        return lax.ppermute(array, "zh", ring(2, 1))

    cross1 = across(along_y(CROSS, True, False))
    cross2 = across(along_y(CROSS, False, True))
    stay = along_y(STAY, True, True)
    part = 512
    columns = pl.BlockSpec((slots, part), lambda j: (0, j))
    shifts = [(dz, dx) for _, dzs, dx in groups for dz in dzs]
    arrays = [a for a, _, _ in groups]
    product = jax.ShapeDtypeStruct((slots, units), F32)
    scratch = [pltpu.VMEM((slots, half), BF16)]
    theirs, whole = call(
        functools.partial(theirs_kernel, shifts),
        (product, jax.ShapeDtypeStruct((units, half), BF16)),
        [SMEM, VMEM, VMEM]
        + [pl.BlockSpec((a.shape[0], part, LANES), lambda j: (0, j, 0)) for a in arrays],
        (columns, VMEM),
        scratch,
        (units // part,),
    )(info, near(stay), near(cross1), *map(far, arrays))
    theirs = lax.ppermute(theirs, "c", ring(2, 1))
    mine = call(
        functools.partial(mine_kernel, shifts, height),
        product,
        [SMEM, VMEM, VMEM, VMEM],
        columns,
        scratch,
        (units // part,),
    )(info, near(stay), near(cross2), near(whole))
    steps = 4
    rows = slots // steps
    tile = (sources // steps, 8, LANES)
    wide = pl.BlockSpec((rows, 2 * units), lambda i, info: (i, 0))
    gates = pl.BlockSpec(tile, lambda i, info: (i % 2, 0, 0))
    grad_pre, score = call(
        finish_kernel,
        (
            jax.ShapeDtypeStruct((slots, 2 * units), BF16),
            jax.ShapeDtypeStruct((sources, 8, LANES), F32),
        ),
        [pl.BlockSpec((rows, units), lambda i, info: (piece(i, info), 0)), VMEM, wide, gates, gates],
        (wide, pl.BlockSpec(tile, lambda i, info: (i, 0, 0))),
        grid=(steps,),
        prefetch=1,
    )(info, mine, near(theirs), saved[0, 0], stay[:, 2 * height :, :], cross2[:, height:, :])
    back = lax.all_to_all(score, EP, split_axis=0, concat_axis=0, tiled=True)
    grad_gate = call(
        home_kernel, jax.ShapeDtypeStruct((routes.shape[1], tokens), F32), [VMEM, VMEM], VMEM
    )(routes_t, back)
    return grad_pre.reshape(saved.shape), grad_gate.T


def solution(mesh):
    fine = Mesh(mesh.devices.reshape(2, 8, 4, 4, 2), ("zh", "y", "zl", "x", "c"))
    sp = ("zl", "x", "c")
    in_specs = (
        P(EP + sp, None),
        P(EP + sp, None),
        P(EP + sp, None),
        P(EP, sp, None, None),
        P(EP, None, sp),
    )
    out_specs = (P(EP, sp, None, None), P(EP + sp, None))
    return jax.shard_map(step, mesh=fine, in_specs=in_specs, out_specs=out_specs, check_vma=False)
```

profile of v0, /device:TPU:1, one launch (start us, length us, event | category | flops | bytes accessed | tf_op | source)
XLA Modules:
  0.0 201.2 jit_solution(12861166868316067539)
XLA Ops:
  0.6 0.1 stack.23.core_ref.info_ref
  0.7 1.5 shard_map.68
  2.2 8.7 %collective-permute-start = (bf16[144,2048]{1,0:T(8,128)(2,1)S(1)}, bf16[144,2048]{1,0:T(8,128)(2,1)S(1)}, u32[]{:S(2)}, u32[]{:S(2)}) collective-permute-start(bf16[144,2048]{1,0:T(8,128)(2,1)S(1)} %get-tuple-element.8), channel_id=1, source_target_pairs={{1,0},{0,1},{3,2},{2,3},{5,4},{4,5},{7,6},{6,7},{9,8},{8,9},{11,10... | collective-permute-start | bytes 1769480 | tf_op jit(solution)/shard_map/ppermute | solution.py:256
  11.0 2.3 %collective-permute-start.3 = (bf16[1,1536,128]{2,1,0:T(8,128)(2,1)}, bf16[1,1536,128]{2,1,0:T(8,128)(2,1)S(1)}, u32[]{:S(2)}, u32[]{:S(2)}) collective-permute-start(bf16[1,1536,128]{2,1,0:T(8,128)(2,1)} %param.9), channel_id=1, source_target_pairs={{8,0},{16,8},{24,16},{0,24},{9,1},{17,9},{25,17},{1,25},{10,2},{18... | collective-permute-start | bytes 1179656 | tf_op jit(solution)/shard_map/ppermute | solution.py:220
  13.3 0.0 collective-permute-done.got_ref
  13.3 0.0 copy-start.11
  13.3 2.0 shard_map.71
  15.3 6.8 %all-to-all-start.2 = ((bf16[8,256,128]{2,1,0:T(8,128)(2,1)}), bf16[8,256,128]{2,1,0:T(8,128)(2,1)S(1)}, u32[]{:S(2)}, u32[]{:S(2)}) async-start(bf16[8,256,128]{2,1,0:T(8,128)(2,1)} %shard_map.71), calls=%async_computation.2 | async-start | bytes 1048576 | tf_op jit(solution)/shard_map/all_to_all | solution.py:268
  22.1 1.9 collective-permute-start.4
  24.0 0.8 constant_dynamic-update-slice_fusion.2
  24.8 0.0 collective-permute-done.3
  24.8 0.8 constant_dynamic-update-slice_fusion.1
  25.6 10.3 %collective-permute-done.4 = bf16[1,1536,128]{2,1,0:T(8,128)(2,1)S(1)} collective-permute-done((bf16[1,1536,128]{2,1,0:T(8,128)(2,1)S(1)}, bf16[1,1536,128]{2,1,0:T(8,128)(2,1)S(1)}, u32[]{:S(2)}, u32[]{:S(2)}) %collective-permute-start.4) | collective-permute-done | bytes 393248 | tf_op jit(solution)/shard_map/ppermute | solution.py:220
  35.9 0.8 constant_dynamic-update-slice_fusion.refs_0_
  36.7 4.4 %collective-permute-start.5 = (bf16[3,1536,128]{2,1,0:T(8,128)(2,1)}, bf16[3,1536,128]{2,1,0:T(8,128)(2,1)}, u32[]{:S(2)}, u32[]{:S(2)}) collective-permute-start(bf16[3,1536,128]{2,1,0:T(8,128)(2,1)} %constant_dynamic-update-slice_fusion.refs_0_), channel_id=1, source_target_pairs={{2,0},{4,2},{6,4},{0,6},{3,1},{5,3},{7,5},{1,7},{10,8},{12,10},{14... | collective-permute-start | bytes 3538952 | tf_op jit(solution)/shard_map/ppermute | solution.py:220
  41.0 2.4 %shard_map.69 = bf16[8,520,128]{2,1,0:T(8,128)(2,1)} custom-call(s32[5]{0:T(128)S(1)} %stack.23.core_ref.info_ref, bf16[144,2048]{1,0:T(8,128)(2,1)S(1)} %collective-permute-done.got_ref, bf16[128,2048]{1,0:T(8,128)(2,1)S(1)} %get-tuple-element.9.keep_ref, s32[8,128]{1,0:T(8,128)} %bitcast.13, bf16[8,128]{1,0:T(8,128)(2,1)} %bitcast.17), custom_call_target="tpu_custom_call" | custom-call | tf_op jit(solution)/shard_map/pallas_call | solution.py:262
  43.4 0.0 all-to-all-done.2
  43.4 0.8 copy-done.4
  44.2 6.4 %all-to-all-start = ((bf16[8,520,128]{2,1,0:T(8,128)(2,1)}), bf16[8,520,128]{2,1,0:T(8,128)(2,1)S(1)}, u32[]{:S(2)}, u32[]{:S(2)}) async-start(bf16[8,520,128]{2,1,0:T(8,128)(2,1)} %shard_map.69), calls=%async_computation | async-start | bytes 2129920 | tf_op jit(solution)/shard_map/all_to_all | solution.py:268
  50.6 2.1 %collective-permute-start.6 = (bf16[3,1536,128]{2,1,0:T(8,128)(2,1)}, bf16[3,1536,128]{2,1,0:T(8,128)(2,1)S(1)}, u32[]{:S(2)}, u32[]{:S(2)}) collective-permute-start(bf16[3,1536,128]{2,1,0:T(8,128)(2,1)} %constant_dynamic-update-slice_fusion.refs_0_), channel_id=1, source_target_pairs={{6,0},{0,2},{2,4},{4,6},{7,1},{1,3},{3,5},{5,7},{14,8},{8,10},{10,... | collective-permute-start | bytes 3538952 | tf_op jit(solution)/shard_map/ppermute | solution.py:220
  52.6 1.9 collective-permute-start.7
  54.6 18.5 %collective-permute-done.7.refs_3_ = bf16[1,1536,128]{2,1,0:T(8,128)(2,1)S(1)} collective-permute-done((bf16[1,1536,128]{2,1,0:T(8,128)(2,1)S(1)}, bf16[1,1536,128]{2,1,0:T(8,128)(2,1)S(1)}, u32[]{:S(2)}, u32[]{:S(2)}) %collective-permute-start.7) | collective-permute-done | bytes 393248 | tf_op jit(solution)/shard_map/ppermute | solution.py:220
  73.1 2.1 %collective-permute-start.9 = (bf16[1,1536,128]{2,1,0:T(8,128)(2,1)S(1)}, bf16[1,1536,128]{2,1,0:T(8,128)(2,1)S(1)}, u32[]{:S(2)}, u32[]{:S(2)}) collective-permute-start(bf16[1,1536,128]{2,1,0:T(8,128)(2,1)S(1)} %collective-permute-done.7.refs_3_), channel_id=1, source_target_pairs={{6,0},{0,2},{2,4},{4,6},{7,1},{1,3},{3,5},{5,7},{14,8},{8,10},{10,... | collective-permute-start | bytes 1179656 | tf_op jit(solution)/shard_map/ppermute | solution.py:220
  75.2 0.0 collective-permute-done.5.refs_1_
  75.2 1.2 slice.16
  76.4 4.4 %collective-permute-start.10 = (bf16[2,1536,128]{2,1,0:T(8,128)(2,1)S(1)}, bf16[2,1536,128]{2,1,0:T(8,128)(2,1)S(1)}, u32[]{:S(2)}, u32[]{:S(2)}) collective-permute-start(bf16[2,1536,128]{2,1,0:T(8,128)(2,1)S(1)} %slice.16), channel_id=1, source_target_pairs={{2,0},{4,2},{6,4},{0,6},{3,1},{5,3},{7,5},{1,7},{10,8},{12,10},{14... | collective-permute-start | bytes 2359304 | tf_op jit(solution)/shard_map/ppermute | solution.py:220
  80.8 7.9 %collective-permute-start.2 = (bf16[8,256,128]{2,1,0:T(8,128)(2,1)S(1)}, bf16[8,256,128]{2,1,0:T(8,128)(2,1)S(1)}, u32[]{:S(2)}, u32[]{:S(2)}) collective-permute-start(bf16[8,256,128]{2,1,0:T(8,128)(2,1)S(1)} %copy-done.5), channel_id=1, source_target_pairs={{256,0},{0,256},{257,1},{1,257},{258,2},{2,258},{259,3},{3,259},{2... | collective-permute-start | bytes 1572872 | tf_op jit(solution)/shard_map/ppermute | solution.py:271
  88.7 3.4 %collective-permute-start.8 = (bf16[1,1536,128]{2,1,0:T(8,128)(2,1)S(1)}, bf16[1,1536,128]{2,1,0:T(8,128)(2,1)S(1)}, u32[]{:S(2)}, u32[]{:S(2)}) collective-permute-start(bf16[1,1536,128]{2,1,0:T(8,128)(2,1)S(1)} %collective-permute-done.7.refs_3_), channel_id=1, source_target_pairs={{2,0},{4,2},{6,4},{0,6},{3,1},{5,3},{7,5},{1,7},{10,8},{12,10},{14... | collective-permute-start | bytes 1179656 | tf_op jit(solution)/shard_map/ppermute | solution.py:220
  92.1 0.0 collective-permute-done.9.refs_5_
  92.1 1.9 collective-permute-start.12
  94.1 0.0 collective-permute-done.6.refs_2_
  94.1 1.9 collective-permute-start.11
  96.0 9.3 %collective-permute-done.8.refs_4_ = bf16[1,1536,128]{2,1,0:T(8,128)(2,1)S(1)} collective-permute-done((bf16[1,1536,128]{2,1,0:T(8,128)(2,1)S(1)}, bf16[1,1536,128]{2,1,0:T(8,128)(2,1)S(1)}, u32[]{:S(2)}, u32[]{:S(2)}) %collective-permute-start.8) | collective-permute-done | bytes 393248 | tf_op jit(solution)/shard_map/ppermute | solution.py:220
  105.3 7.4 %collective-permute-done.11.refs_7_ = bf16[1,1536,128]{2,1,0:T(8,128)(2,1)S(1)} collective-permute-done((bf16[1,1536,128]{2,1,0:T(8,128)(2,1)S(1)}, bf16[1,1536,128]{2,1,0:T(8,128)(2,1)S(1)}, u32[]{:S(2)}, u32[]{:S(2)}) %collective-permute-start.11) | collective-permute-done | bytes 393248 | tf_op jit(solution)/shard_map/ppermute | solution.py:220
  112.8 0.7 copy-done.10
  113.5 0.9 copy-done.3
  114.4 5.1 %shard_map.72 = (f32[256,1536]{1,0:T(8,128)S(1)}, bf16[1536,2048]{1,0:T(8,128)(2,1)S(1)}) custom-call(s32[5]{0:T(128)S(1)} %stack.23.core_ref.info_ref, bf16[8,520,128]{2,1,0:T(8,128)(2,1)S(1)} %all-to-all-done.stay_ref, bf16[8,256,128]{2,1,0:T(8,128)(2,1)S(1)} %collective-permute-done.2.cross_ref, ...), custom_call_target="tpu_custom_call" | custom-call | tf_op jit(solution)/shard_map/pallas_call | solution.py:282
  119.4 4.4 %collective-permute-start.13 = (f32[256,1536]{1,0:T(8,128)S(1)}, f32[256,1536]{1,0:T(8,128)S(1)}, u32[]{:S(2)}, u32[]{:S(2)}) collective-permute-start(f32[256,1536]{1,0:T(8,128)S(1)} %get-tuple-element.11), channel_id=1, source_target_pairs={{1,0},{0,1},{3,2},{2,3},{5,4},{4,5},{7,6},{6,7},{9,8},{8,9},{11,10... | collective-permute-start | bytes 4718600 | tf_op jit(solution)/shard_map/ppermute | solution.py:291
  123.8 1.1 shard_map.70
  125.0 24.7 %all_to_all.20 = bf16[8,264,128]{2,1,0:T(8,128)(2,1)S(1)} all-to-all(bf16[8,264,128]{2,1,0:T(8,128)(2,1)S(1)} %shard_map.70), channel_id=1, replica_groups=mesh['zh'=2,'y'=8,'zl'=4,'x'=4,'c'=2] {'y'}, dimensions={0} | all-to-all | bytes 1081344 | tf_op jit(solution)/shard_map/all_to_all | solution.py:268
  149.6 3.2 %collective-permute-start.1 = (bf16[8,264,128]{2,1,0:T(8,128)(2,1)S(1)}, bf16[8,264,128]{2,1,0:T(8,128)(2,1)S(1)}, u32[]{:S(2)}, u32[]{:S(2)}) collective-permute-start(bf16[8,264,128]{2,1,0:T(8,128)(2,1)S(1)} %all_to_all.20), channel_id=1, source_target_pairs={{256,0},{0,256},{257,1},{1,257},{258,2},{2,258},{259,3},{3,259},{2... | collective-permute-start | bytes 1622024 | tf_op jit(solution)/shard_map/ppermute | solution.py:271
  152.8 26.5 %collective-permute-done.1.cross_ref = bf16[8,264,128]{2,1,0:T(8,128)(2,1)S(1)} collective-permute-done((bf16[8,264,128]{2,1,0:T(8,128)(2,1)S(1)}, bf16[8,264,128]{2,1,0:T(8,128)(2,1)S(1)}, u32[]{:S(2)}, u32[]{:S(2)}) %collective-permute-start.1) | collective-permute-done | bytes 540704 | tf_op jit(solution)/shard_map/ppermute | solution.py:271
  179.3 3.3 %shard_map.73.mine_ref = f32[256,1536]{1,0:T(8,128)S(1)} custom-call(s32[5]{0:T(128)S(1)} %stack.23.core_ref.info_ref, bf16[8,520,128]{2,1,0:T(8,128)(2,1)S(1)} %all-to-all-done.stay_ref, bf16[8,264,128]{2,1,0:T(8,128)(2,1)S(1)} %collective-permute-done.1.cross_ref, bf16[1536,2048]{1,0:T(8,128)(2,1)S(1)} %get-tuple-element.10.whole_ref), custom_call_target="tpu_custom_call" | custom-call | tf_op jit(solution)/shard_map/pallas_call | solution.py:292
  182.6 0.0 collective-permute-done.13.theirs_ref
  182.6 0.0 copy-start.1
  182.6 3.1 %shard_map.74 = (bf16[256,3072]{1,0:T(8,128)(2,1)}, f32[16,8,128]{2,1,0:T(8,128)S(1)}) custom-call(s32[5]{0:T(128)S(1)} %stack.23.core_ref.info_ref, f32[256,1536]{1,0:T(8,128)S(1)} %shard_map.73.mine_ref, f32[256,1536]{1,0:T(8,128)S(1)} %collective-permute-done.13.theirs_ref, bf16[256,3072]{1,0:T(8,128)(2,1)S(1)} %bitcast.10, ...), custom_call_target="tpu_custom_call" | custom-call | tf_op jit(solution)/shard_map/pallas_call | solution.py:305
  185.7 14.8 %all_to_all.21.back_ref = f32[16,8,128]{2,1,0:T(8,128)S(1)} all-to-all(f32[16,8,128]{2,1,0:T(8,128)S(1)} %get-tuple-element.13), channel_id=1, replica_groups=mesh['zh'=2,'y'=8,'zl'=4,'x'=4,'c'=2] {'zh','y'}, dimensions={0} | all-to-all | bytes 131072 | tf_op jit(solution)/shard_map/all_to_all | solution.py:316
  200.4 0.8 shard_map.75
  (26 shorter events, 0.1 us)
Async XLA Ops:
  2.2 11.0 %collective-permute-start = (bf16[144,2048]{1,0:T(8,128)(2,1)S(1)}, bf16[144,2048]{1,0:T(8,128)(2,1)S(1)}, u32[]{:S(2)}, u32[]{:S(2)}) collective-permute-start(bf16[144,2048]{1,0:T(8,128)(2,1)S(1)} %get-tuple-element.8), channel_id=1, source_target_pairs={{1,0},{0,1},{3,2},{2,3},{5,4},{4,5},{7,6},{6,7},{9,8},{8,9},{11,10... | collective-permute-start | bytes 1769480 | tf_op jit(solution)/shard_map/ppermute | solution.py:256
  11.0 13.8 %collective-permute-start.3 = (bf16[1,1536,128]{2,1,0:T(8,128)(2,1)}, bf16[1,1536,128]{2,1,0:T(8,128)(2,1)S(1)}, u32[]{:S(2)}, u32[]{:S(2)}) collective-permute-start(bf16[1,1536,128]{2,1,0:T(8,128)(2,1)} %param.9), channel_id=1, source_target_pairs={{8,0},{16,8},{24,16},{0,24},{9,1},{17,9},{25,17},{1,25},{10,2},{18... | collective-permute-start | bytes 1179656 | tf_op jit(solution)/shard_map/ppermute | solution.py:220
  13.3 8.8 %copy-start.11 = (bf16[1,1536,128]{2,1,0:T(8,128)(2,1)S(1)}, bf16[1,1536,128]{2,1,0:T(8,128)(2,1)}, u32[]{:S(2)}) copy-start(bf16[1,1536,128]{2,1,0:T(8,128)(2,1)} %param.9) | copy-start | bytes 1179652
  15.3 28.1 %all-to-all-start.2 = ((bf16[8,256,128]{2,1,0:T(8,128)(2,1)}), bf16[8,256,128]{2,1,0:T(8,128)(2,1)S(1)}, u32[]{:S(2)}, u32[]{:S(2)}) async-start(bf16[8,256,128]{2,1,0:T(8,128)(2,1)} %shard_map.71), calls=%async_computation.2 | async-start | bytes 1048576 | tf_op jit(solution)/shard_map/all_to_all | solution.py:268
  22.1 13.8 %collective-permute-start.4 = (bf16[1,1536,128]{2,1,0:T(8,128)(2,1)S(1)}, bf16[1,1536,128]{2,1,0:T(8,128)(2,1)S(1)}, u32[]{:S(2)}, u32[]{:S(2)}) collective-permute-start(bf16[1,1536,128]{2,1,0:T(8,128)(2,1)S(1)} %copy-done.11), channel_id=1, source_target_pairs={{24,0},{0,8},{8,16},{16,24},{25,1},{1,9},{9,17},{17,25},{26,2},{2,... | collective-permute-start | bytes 1179656 | tf_op jit(solution)/shard_map/ppermute | solution.py:220
  36.7 38.5 %collective-permute-start.5 = (bf16[3,1536,128]{2,1,0:T(8,128)(2,1)}, bf16[3,1536,128]{2,1,0:T(8,128)(2,1)}, u32[]{:S(2)}, u32[]{:S(2)}) collective-permute-start(bf16[3,1536,128]{2,1,0:T(8,128)(2,1)} %constant_dynamic-update-slice_fusion.refs_0_), channel_id=1, source_target_pairs={{2,0},{4,2},{6,4},{0,6},{3,1},{5,3},{7,5},{1,7},{10,8},{12,10},{14... | collective-permute-start | bytes 3538952 | tf_op jit(solution)/shard_map/ppermute | solution.py:220
  43.4 0.8 copy-start.4
  44.2 69.3 %all-to-all-start = ((bf16[8,520,128]{2,1,0:T(8,128)(2,1)}), bf16[8,520,128]{2,1,0:T(8,128)(2,1)S(1)}, u32[]{:S(2)}, u32[]{:S(2)}) async-start(bf16[8,520,128]{2,1,0:T(8,128)(2,1)} %shard_map.69), calls=%async_computation | async-start | bytes 2129920 | tf_op jit(solution)/shard_map/all_to_all | solution.py:268
  50.6 30.2 %copy-start.5 = (bf16[8,256,128]{2,1,0:T(8,128)(2,1)S(1)}, bf16[8,256,128]{2,1,0:T(8,128)(2,1)}, u32[]{:S(2)}) copy-start(bf16[8,256,128]{2,1,0:T(8,128)(2,1)} %copy-done.4) | copy-start | bytes 1572868
  50.6 43.5 %collective-permute-start.6 = (bf16[3,1536,128]{2,1,0:T(8,128)(2,1)}, bf16[3,1536,128]{2,1,0:T(8,128)(2,1)S(1)}, u32[]{:S(2)}, u32[]{:S(2)}) collective-permute-start(bf16[3,1536,128]{2,1,0:T(8,128)(2,1)} %constant_dynamic-update-slice_fusion.refs_0_), channel_id=1, source_target_pairs={{6,0},{0,2},{2,4},{4,6},{7,1},{1,3},{3,5},{5,7},{14,8},{8,10},{10,... | collective-permute-start | bytes 3538952 | tf_op jit(solution)/shard_map/ppermute | solution.py:220
  52.6 20.5 %collective-permute-start.7 = (bf16[1,1536,128]{2,1,0:T(8,128)(2,1)S(1)}, bf16[1,1536,128]{2,1,0:T(8,128)(2,1)S(1)}, u32[]{:S(2)}, u32[]{:S(2)}) collective-permute-start(bf16[1,1536,128]{2,1,0:T(8,128)(2,1)S(1)} %copy-done.11), channel_id=1, source_target_pairs={{16,0},{24,8},{0,16},{8,24},{17,1},{25,9},{1,17},{9,25},{18,2},{26... | collective-permute-start | bytes 1179656 | tf_op jit(solution)/shard_map/ppermute | solution.py:220
  73.1 39.6 %copy-start.6 = (bf16[1,1536,128]{2,1,0:T(8,128)(2,1)}, bf16[1,1536,128]{2,1,0:T(8,128)(2,1)S(1)}, u32[]{:S(2)}) copy-start(bf16[1,1536,128]{2,1,0:T(8,128)(2,1)S(1)} %collective-permute-done.7.refs_3_) | copy-start | bytes 1179652
  73.1 19.0 %collective-permute-start.9 = (bf16[1,1536,128]{2,1,0:T(8,128)(2,1)S(1)}, bf16[1,1536,128]{2,1,0:T(8,128)(2,1)S(1)}, u32[]{:S(2)}, u32[]{:S(2)}) collective-permute-start(bf16[1,1536,128]{2,1,0:T(8,128)(2,1)S(1)} %collective-permute-done.7.refs_3_), channel_id=1, source_target_pairs={{6,0},{0,2},{2,4},{4,6},{7,1},{1,3},{3,5},{5,7},{14,8},{8,10},{10,... | collective-permute-start | bytes 1179656 | tf_op jit(solution)/shard_map/ppermute | solution.py:220
  76.4 37.1 %collective-permute-start.10 = (bf16[2,1536,128]{2,1,0:T(8,128)(2,1)S(1)}, bf16[2,1536,128]{2,1,0:T(8,128)(2,1)S(1)}, u32[]{:S(2)}, u32[]{:S(2)}) collective-permute-start(bf16[2,1536,128]{2,1,0:T(8,128)(2,1)S(1)} %slice.16), channel_id=1, source_target_pairs={{2,0},{4,2},{6,4},{0,6},{3,1},{5,3},{7,5},{1,7},{10,8},{12,10},{14... | collective-permute-start | bytes 2359304 | tf_op jit(solution)/shard_map/ppermute | solution.py:220
  80.8 31.9 %collective-permute-start.2 = (bf16[8,256,128]{2,1,0:T(8,128)(2,1)S(1)}, bf16[8,256,128]{2,1,0:T(8,128)(2,1)S(1)}, u32[]{:S(2)}, u32[]{:S(2)}) collective-permute-start(bf16[8,256,128]{2,1,0:T(8,128)(2,1)S(1)} %copy-done.5), channel_id=1, source_target_pairs={{256,0},{0,256},{257,1},{1,257},{258,2},{2,258},{259,3},{3,259},{2... | collective-permute-start | bytes 1572872 | tf_op jit(solution)/shard_map/ppermute | solution.py:271
  88.7 16.6 %collective-permute-start.8 = (bf16[1,1536,128]{2,1,0:T(8,128)(2,1)S(1)}, bf16[1,1536,128]{2,1,0:T(8,128)(2,1)S(1)}, u32[]{:S(2)}, u32[]{:S(2)}) collective-permute-start(bf16[1,1536,128]{2,1,0:T(8,128)(2,1)S(1)} %collective-permute-done.7.refs_3_), channel_id=1, source_target_pairs={{2,0},{4,2},{6,4},{0,6},{3,1},{5,3},{7,5},{1,7},{10,8},{12,10},{14... | collective-permute-start | bytes 1179656 | tf_op jit(solution)/shard_map/ppermute | solution.py:220
  92.1 20.6 %copy-start.7 = (bf16[1,1536,128]{2,1,0:T(8,128)(2,1)}, bf16[1,1536,128]{2,1,0:T(8,128)(2,1)S(1)}, u32[]{:S(2)}) copy-start(bf16[1,1536,128]{2,1,0:T(8,128)(2,1)S(1)} %collective-permute-done.9.refs_5_) | copy-start | bytes 1179652
  92.1 13.2 %collective-permute-start.12 = (bf16[1,1536,128]{2,1,0:T(8,128)(2,1)S(1)}, bf16[1,1536,128]{2,1,0:T(8,128)(2,1)S(1)}, u32[]{:S(2)}, u32[]{:S(2)}) collective-permute-start(bf16[1,1536,128]{2,1,0:T(8,128)(2,1)S(1)} %collective-permute-done.9.refs_5_), channel_id=1, source_target_pairs={{6,0},{0,2},{2,4},{4,6},{7,1},{1,3},{3,5},{5,7},{14,8},{8,10},{10,... | collective-permute-start | bytes 1179656 | tf_op jit(solution)/shard_map/ppermute | solution.py:220
  94.1 18.7 %copy-start.2 = (bf16[3,1536,128]{2,1,0:T(8,128)(2,1)}, bf16[3,1536,128]{2,1,0:T(8,128)(2,1)S(1)}, u32[]{:S(2)}) copy-start(bf16[3,1536,128]{2,1,0:T(8,128)(2,1)S(1)} %collective-permute-done.6.refs_2_) | copy-start | bytes 3538948
  94.1 18.6 %collective-permute-start.11 = (bf16[1,1536,128]{2,1,0:T(8,128)(2,1)S(1)}, bf16[1,1536,128]{2,1,0:T(8,128)(2,1)S(1)}, u32[]{:S(2)}, u32[]{:S(2)}) collective-permute-start(bf16[1,1536,128]{2,1,0:T(8,128)(2,1)S(1)} %slice.17), channel_id=1, source_target_pairs={{6,0},{0,2},{2,4},{4,6},{7,1},{1,3},{3,5},{5,7},{14,8},{8,10},{10,... | collective-permute-start | bytes 1179656 | tf_op jit(solution)/shard_map/ppermute | solution.py:220
  105.3 7.4 %copy-start.8 = (bf16[1,1536,128]{2,1,0:T(8,128)(2,1)}, bf16[1,1536,128]{2,1,0:T(8,128)(2,1)S(1)}, u32[]{:S(2)}) copy-start(bf16[1,1536,128]{2,1,0:T(8,128)(2,1)S(1)} %collective-permute-done.8.refs_4_) | copy-start | bytes 1179652
  105.3 7.4 %copy-start.9 = (bf16[1,1536,128]{2,1,0:T(8,128)(2,1)}, bf16[1,1536,128]{2,1,0:T(8,128)(2,1)S(1)}, u32[]{:S(2)}) copy-start(bf16[1,1536,128]{2,1,0:T(8,128)(2,1)S(1)} %collective-permute-done.12.refs_8_) | copy-start | bytes 1179652
  112.7 0.8 copy-start.10
  113.5 0.9 copy-start.3
  119.4 63.2 %collective-permute-start.13 = (f32[256,1536]{1,0:T(8,128)S(1)}, f32[256,1536]{1,0:T(8,128)S(1)}, u32[]{:S(2)}, u32[]{:S(2)}) collective-permute-start(f32[256,1536]{1,0:T(8,128)S(1)} %get-tuple-element.11), channel_id=1, source_target_pairs={{1,0},{0,1},{3,2},{2,3},{5,4},{4,5},{7,6},{6,7},{9,8},{8,9},{11,10... | collective-permute-start | bytes 4718600 | tf_op jit(solution)/shard_map/ppermute | solution.py:291
  149.6 29.7 %collective-permute-start.1 = (bf16[8,264,128]{2,1,0:T(8,128)(2,1)S(1)}, bf16[8,264,128]{2,1,0:T(8,128)(2,1)S(1)}, u32[]{:S(2)}, u32[]{:S(2)}) collective-permute-start(bf16[8,264,128]{2,1,0:T(8,128)(2,1)S(1)} %all_to_all.20), channel_id=1, source_target_pairs={{256,0},{0,256},{257,1},{1,257},{258,2},{2,258},{259,3},{3,259},{2... | collective-permute-start | bytes 1622024 | tf_op jit(solution)/shard_map/ppermute | solution.py:271
  179.3 3.3 %copy-start = (bf16[1,1,256,3072]{3,2,1,0:T(8,128)(2,1)S(1)}, bf16[1,1,256,3072]{3,2,1,0:T(8,128)(2,1)}, u32[]{:S(2)}) copy-start(bf16[1,1,256,3072]{3,2,1,0:T(8,128)(2,1)} %param.8) | copy-start | bytes 4718596
  182.6 17.8 %copy-start.1 = (s32[128,8]{0,1:T(8,128)S(1)}, s32[128,8]{0,1:T(8,128)}, u32[]{:S(2)}) copy-start(s32[128,8]{0,1:T(8,128)} %param.6) | copy-start | bytes 12292
where the time goes:
time: 203 us; the launch traced here: 201 us
  waiting for transfers between devices  72 us (35%)
  starting transfers between devices  63.7 us (31%)
  blocking collectives  39.4 us (19%)
  Pallas kernels  19.1 us (9%)
  local copies, waits for them, and re-layouts  6.03 us (3%)
    ppermute x10, waiting for transfers between devices, permute(): return lax.ppermute(array, axis, ring(4, shift))  45.5 us
    ppermute x2, waiting for transfers between devices, across(): return lax.ppermute(array, 'zh', ring(2, 1))  26.5 us
    ppermute x10, starting transfers between devices, permute(): return lax.ppermute(array, axis, ring(4, shift))  26.2 us
    all_to_all x1, blocking collectives, along_y(): return lax.all_to_all(array, 'y', split_axis=0, concat_axis=0, tiled=True)  24.7 us
    all_to_all x1, blocking collectives, step(): back = lax.all_to_all(score, EP, split_axis=0, concat_axis=0, tiled=True)  14.8 us
    all_to_all x2, starting transfers between devices, along_y(): return lax.all_to_all(array, 'y', split_axis=0, concat_axis=0, tiled=True)  13.2 us
    ppermute x2, starting transfers between devices, across(): return lax.ppermute(array, 'zh', ring(2, 1))  11.1 us
    ppermute x1, starting transfers between devices, step(): got = lax.ppermute(send, 'c', ring(2, 1))  8.74 us
  transfers between devices with their start and end apart: 16, of which 5 were waited for; matrix products, arithmetic and copies ran while one was open for 2% of the time, Pallas kernels for 4%

commit v1 on v0

--- a/solution.py
+++ b/solution.py
@@ -224,13 +224,12 @@
     z1, z3, z2 = (permute(block, "zl", r) for r in (1, 3, 2))
     trio = jnp.concatenate([block, z1, z3], axis=0)
     g1, g3 = permute(trio, "x", 1), permute(trio, "x", 3)
-    h1, h3 = permute(z2, "x", 1), permute(z2, "x", 3)
-    f1 = permute(g1[:2], "x", 1)
-    f3 = permute(g3[2:], "x", 3)
-    f2 = permute(h3, "x", 3)
-    groups = [(trio, (0, 1, 3), 0), (g1, (0, 1, 3), 1), (g3, (0, 1, 3), 3)]
-    groups += [(z2, (2,), 0), (h1, (2,), 1), (h3, (2,), 3)]
-    return groups + [(f1, (0, 1), 2), (f3, (3,), 2), (f2, (2,), 2)]
+    e2 = permute(z2, "x", 2)
+    f1 = permute(jnp.concatenate([g1[:2], z2], axis=0), "x", 1)
+    f3 = permute(jnp.concatenate([g3[2:], z2], axis=0), "x", 3)
+    groups = [(a, [(dz, dx) for dz in (0, 1, 3)]) for a, dx in ((trio, 0), (g1, 1), (g3, 3))]
+    groups += [(z2, [(2, 0)]), (e2, [(2, 2)])]
+    return groups + [(f1, [(0, 2), (1, 2), (2, 1)]), (f3, [(3, 2), (2, 3)])]
 
 
 def step(grad_out, routes, gate, saved, w_down):
@@ -275,8 +274,8 @@
     stay = along_y(STAY, True, True)
     part = 512
     columns = pl.BlockSpec((slots, part), lambda j: (0, j))
-    shifts = [(dz, dx) for _, dzs, dx in groups for dz in dzs]
-    arrays = [a for a, _, _ in groups]
+    shifts = [pair for _, pairs in groups for pair in pairs]
+    arrays = [a for a, _ in groups]
     product = jax.ShapeDtypeStruct((slots, units), F32)
     scratch = [pltpu.VMEM((slots, half), BF16)]
     theirs, whole = call(

time: 203 us -> 199 us (0.980)
  the two profiles are of different devices: /device:TPU:1 before, /device:TPU:64 now
where the time goes in v1:
time: 199 us; the launch traced here: 198 us
  starting transfers between devices  63.6 us (32%)
  waiting for transfers between devices  57.8 us (29%)
  blocking collectives  49.9 us (25%)
  Pallas kernels  19.1 us (10%)
  local copies, waits for them, and re-layouts  6 us (3%)
    ppermute x8, waiting for transfers between devices, permute(): return lax.ppermute(array, axis, ring(4, shift))  33.7 us
    ppermute x8, starting transfers between devices, permute(): return lax.ppermute(array, axis, ring(4, shift))  33.6 us
    all_to_all x1, blocking collectives, along_y(): return lax.all_to_all(array, 'y', split_axis=0, concat_axis=0, tiled=True)  25.1 us
    all_to_all x1, blocking collectives, step(): back = lax.all_to_all(score, EP, split_axis=0, concat_axis=0, tiled=True)  24.7 us
    ppermute x2, waiting for transfers between devices, across(): return lax.ppermute(array, 'zh', ring(2, 1))  18.6 us
    ppermute x2, starting transfers between devices, across(): return lax.ppermute(array, 'zh', ring(2, 1))  15.5 us
    all_to_all x2, starting transfers between devices, along_y(): return lax.all_to_all(array, 'y', split_axis=0, concat_axis=0, tiled=True)  10.7 us
    pallas_call x3, Pallas kernels, along_y(): call(functools.partial(dispatch_kernel, side, theirs, mine), jax.ShapeDty...  5.46 us
  transfers between devices with their start and end apart: 14, of which 9 were waited for; matrix products, arithmetic and copies ran while one was open for 3% of the time, Pallas kernels for 5%

profile of v1, /device:TPU:64, one launch (start us, length us, event | category | flops | bytes accessed | tf_op | source)
XLA Modules:
  0.0 198.5 jit_solution(15134847223802742435)
XLA Ops:
  0.6 0.0 copy-start.8
  0.6 7.0 %collective-permute-start.3 = (bf16[1,1536,128]{2,1,0:T(8,128)(2,1)}, bf16[1,1536,128]{2,1,0:T(8,128)(2,1)}, u32[]{:S(2)}, u32[]{:S(2)}) collective-permute-start(bf16[1,1536,128]{2,1,0:T(8,128)(2,1)} %param.9), channel_id=1, source_target_pairs={{8,0},{16,8},{24,16},{0,24},{9,1},{17,9},{25,17},{1,25},{10,2},{18... | collective-permute-start | bytes 1179656 | tf_op jit(solution)/shard_map/ppermute | solution.py:220
  7.7 0.1 stack.23.core_ref.info_ref
  7.8 1.5 shard_map.68
  9.3 1.9 collective-permute-start
  11.2 1.9 collective-permute-start.4
  13.2 1.3 collective-permute-done.3
  14.5 1.0 constant_dynamic-update-slice_fusion.1
  15.5 1.9 shard_map.71
  17.5 7.1 %all-to-all-start.2 = ((bf16[8,256,128]{2,1,0:T(8,128)(2,1)}), bf16[8,256,128]{2,1,0:T(8,128)(2,1)S(1)}, u32[]{:S(2)}, u32[]{:S(2)}) async-start(bf16[8,256,128]{2,1,0:T(8,128)(2,1)} %shard_map.71), calls=%async_computation.2 | async-start | bytes 1048576 | tf_op jit(solution)/shard_map/all_to_all | solution.py:267
  24.6 1.3 collective-permute-done.4
  25.9 1.0 constant_dynamic-update-slice_fusion.refs_0_
  26.9 0.0 copy-start.3
  27.0 4.7 %collective-permute-start.5 = (bf16[3,1536,128]{2,1,0:T(8,128)(2,1)S(1)}, bf16[3,1536,128]{2,1,0:T(8,128)(2,1)}, u32[]{:S(2)}, u32[]{:S(2)}) collective-permute-start(bf16[3,1536,128]{2,1,0:T(8,128)(2,1)S(1)} %constant_dynamic-update-slice_fusion.refs_0_), channel_id=1, source_target_pairs={{2,0},{4,2},{6,4},{0,6},{3,1},{5,3},{7,5},{1,7},{10,8},{12,10},{14... | collective-permute-start | bytes 3538952 | tf_op jit(solution)/shard_map/ppermute | solution.py:220
  31.7 1.9 collective-permute-start.6
  33.6 2.4 %shard_map.69 = bf16[8,520,128]{2,1,0:T(8,128)(2,1)} custom-call(s32[5]{0:T(128)S(1)} %stack.23.core_ref.info_ref, bf16[144,2048]{1,0:T(8,128)(2,1)S(1)} %collective-permute-done.got_ref, bf16[128,2048]{1,0:T(8,128)(2,1)S(1)} %get-tuple-element.9.keep_ref, s32[8,128]{1,0:T(8,128)} %bitcast.13, bf16[8,128]{1,0:T(8,128)(2,1)} %bitcast.17), custom_call_target="tpu_custom_call" | custom-call | tf_op jit(solution)/shard_map/pallas_call | solution.py:261
  36.0 5.5 %all-to-all-done.2 = bf16[8,256,128]{2,1,0:T(8,128)(2,1)S(1)} async-done(((bf16[8,256,128]{2,1,0:T(8,128)(2,1)}), bf16[8,256,128]{2,1,0:T(8,128)(2,1)S(1)}, u32[]{:S(2)}, u32[]{:S(2)}) %all-to-all-start.2) | async-done | bytes 524320 | tf_op jit(solution)/shard_map/all_to_all | solution.py:267
  41.5 0.8 copy-done.5
  42.3 3.6 %all-to-all-start = ((bf16[8,520,128]{2,1,0:T(8,128)(2,1)}), bf16[8,520,128]{2,1,0:T(8,128)(2,1)S(1)}, u32[]{:S(2)}, u32[]{:S(2)}) async-start(bf16[8,520,128]{2,1,0:T(8,128)(2,1)} %shard_map.69), calls=%async_computation | async-start | bytes 2129920 | tf_op jit(solution)/shard_map/all_to_all | solution.py:267
  45.9 7.0 %collective-permute-start.7 = (bf16[1,1536,128]{2,1,0:T(8,128)(2,1)}, bf16[1,1536,128]{2,1,0:T(8,128)(2,1)S(1)}, u32[]{:S(2)}, u32[]{:S(2)}) collective-permute-start(bf16[1,1536,128]{2,1,0:T(8,128)(2,1)} %param.9), channel_id=1, source_target_pairs={{16,0},{24,8},{0,16},{8,24},{17,1},{25,9},{1,17},{9,25},{18,2},{26... | collective-permute-start | bytes 1179656 | tf_op jit(solution)/shard_map/ppermute | solution.py:220
  52.9 3.1 %collective-permute-done.5.refs_1_ = bf16[3,1536,128]{2,1,0:T(8,128)(2,1)} collective-permute-done((bf16[3,1536,128]{2,1,0:T(8,128)(2,1)S(1)}, bf16[3,1536,128]{2,1,0:T(8,128)(2,1)}, u32[]{:S(2)}, u32[]{:S(2)}) %collective-permute-start.5) | collective-permute-done | bytes 1179680 | tf_op jit(solution)/shard_map/ppermute | solution.py:220
  56.0 1.2 slice.16
  57.2 9.6 %collective-permute-done.7.refs_3_ = bf16[1,1536,128]{2,1,0:T(8,128)(2,1)S(1)} collective-permute-done((bf16[1,1536,128]{2,1,0:T(8,128)(2,1)}, bf16[1,1536,128]{2,1,0:T(8,128)(2,1)S(1)}, u32[]{:S(2)}, u32[]{:S(2)}) %collective-permute-start.7) | collective-permute-done | bytes 393248 | tf_op jit(solution)/shard_map/ppermute | solution.py:220
  66.8 1.2 pad_maximum_fusion
  68.0 4.8 %collective-permute-start.9 = (bf16[3,1536,128]{2,1,0:T(8,128)(2,1)}, bf16[3,1536,128]{2,1,0:T(8,128)(2,1)}, u32[]{:S(2)}, u32[]{:S(2)}) collective-permute-start(bf16[3,1536,128]{2,1,0:T(8,128)(2,1)} %pad_maximum_fusion), channel_id=1, source_target_pairs={{2,0},{4,2},{6,4},{0,6},{3,1},{5,3},{7,5},{1,7},{10,8},{12,10},{14... | collective-permute-start | bytes 3538952 | tf_op jit(solution)/shard_map/ppermute | solution.py:220
  72.8 0.0 collective-permute-done.6.refs_2_
  72.8 1.0 slice.17
  73.8 0.1 pad_maximum_fusion.1
  73.9 1.9 collective-permute-start.10
  75.9 7.8 %collective-permute-start.2 = (bf16[8,256,128]{2,1,0:T(8,128)(2,1)S(1)}, bf16[8,256,128]{2,1,0:T(8,128)(2,1)S(1)}, u32[]{:S(2)}, u32[]{:S(2)}) collective-permute-start(bf16[8,256,128]{2,1,0:T(8,128)(2,1)S(1)} %copy-done.6), channel_id=1, source_target_pairs={{256,0},{0,256},{257,1},{1,257},{258,2},{2,258},{259,3},{3,259},{2... | collective-permute-start | bytes 1572872 | tf_op jit(solution)/shard_map/ppermute | solution.py:270
  83.7 4.2 %collective-permute-start.8 = (bf16[1,1536,128]{2,1,0:T(8,128)(2,1)S(1)}, bf16[1,1536,128]{2,1,0:T(8,128)(2,1)S(1)}, u32[]{:S(2)}, u32[]{:S(2)}) collective-permute-start(bf16[1,1536,128]{2,1,0:T(8,128)(2,1)S(1)} %collective-permute-done.7.refs_3_), channel_id=1, source_target_pairs={{4,0},{6,2},{0,4},{2,6},{5,1},{7,3},{1,5},{3,7},{12,8},{14,10},{8,... | collective-permute-start | bytes 1179656 | tf_op jit(solution)/shard_map/ppermute | solution.py:220
  87.9 15.9 %collective-permute-done.8.refs_4_ = bf16[1,1536,128]{2,1,0:T(8,128)(2,1)S(1)} collective-permute-done((bf16[1,1536,128]{2,1,0:T(8,128)(2,1)S(1)}, bf16[1,1536,128]{2,1,0:T(8,128)(2,1)S(1)}, u32[]{:S(2)}, u32[]{:S(2)}) %collective-permute-start.8) | collective-permute-done | bytes 393248 | tf_op jit(solution)/shard_map/ppermute | solution.py:220
  103.8 0.7 copy-done.7
  104.5 0.1 collective-permute-done.10.refs_6_
  104.6 0.0 all-to-all-done.stay_ref
  104.7 2.3 %collective-permute-done.9.refs_5_ = bf16[3,1536,128]{2,1,0:T(8,128)(2,1)} collective-permute-done((bf16[3,1536,128]{2,1,0:T(8,128)(2,1)}, bf16[3,1536,128]{2,1,0:T(8,128)(2,1)}, u32[]{:S(2)}, u32[]{:S(2)}) %collective-permute-start.9) | collective-permute-done | bytes 1179680 | tf_op jit(solution)/shard_map/ppermute | solution.py:220
  107.0 5.1 %shard_map.72 = (f32[256,1536]{1,0:T(8,128)S(1)}, bf16[1536,2048]{1,0:T(8,128)(2,1)S(1)}) custom-call(s32[5]{0:T(128)S(1)} %stack.23.core_ref.info_ref, bf16[8,520,128]{2,1,0:T(8,128)(2,1)S(1)} %all-to-all-done.stay_ref, bf16[8,256,128]{2,1,0:T(8,128)(2,1)S(1)} %collective-permute-done.2.cross_ref, bf16[3,1536,128]{2,1,0:T(8,128)(2,1)} %copy-done.3, ...), custom_call_target="tpu_custom_call" | custom-call | tf_op jit(solution)/shard_map/pallas_call | solution.py:281
  112.0 1.9 collective-permute-start.11
  114.0 1.1 shard_map.70
  115.1 25.1 %all_to_all.20 = bf16[8,264,128]{2,1,0:T(8,128)(2,1)S(1)} all-to-all(bf16[8,264,128]{2,1,0:T(8,128)(2,1)S(1)} %shard_map.70), channel_id=1, replica_groups=mesh['zh'=2,'y'=8,'zl'=4,'x'=4,'c'=2] {'y'}, dimensions={0} | all-to-all | bytes 1081344 | tf_op jit(solution)/shard_map/all_to_all | solution.py:267
  140.2 7.8 %collective-permute-start.1 = (bf16[8,264,128]{2,1,0:T(8,128)(2,1)S(1)}, bf16[8,264,128]{2,1,0:T(8,128)(2,1)S(1)}, u32[]{:S(2)}, u32[]{:S(2)}) collective-permute-start(bf16[8,264,128]{2,1,0:T(8,128)(2,1)S(1)} %all_to_all.20), channel_id=1, source_target_pairs={{256,0},{0,256},{257,1},{1,257},{258,2},{2,258},{259,3},{3,259},{2... | collective-permute-start | bytes 1622024 | tf_op jit(solution)/shard_map/ppermute | solution.py:270
  148.0 18.6 %collective-permute-done.1.cross_ref = bf16[8,264,128]{2,1,0:T(8,128)(2,1)S(1)} collective-permute-done((bf16[8,264,128]{2,1,0:T(8,128)(2,1)S(1)}, bf16[8,264,128]{2,1,0:T(8,128)(2,1)S(1)}, u32[]{:S(2)}, u32[]{:S(2)}) %collective-permute-start.1) | collective-permute-done | bytes 540704 | tf_op jit(solution)/shard_map/ppermute | solution.py:270
  166.6 3.3 %shard_map.73.mine_ref = f32[256,1536]{1,0:T(8,128)S(1)} custom-call(s32[5]{0:T(128)S(1)} %stack.23.core_ref.info_ref, bf16[8,520,128]{2,1,0:T(8,128)(2,1)S(1)} %all-to-all-done.stay_ref, bf16[8,264,128]{2,1,0:T(8,128)(2,1)S(1)} %collective-permute-done.1.cross_ref, bf16[1536,2048]{1,0:T(8,128)(2,1)S(1)} %get-tuple-element.10.whole_ref), custom_call_target="tpu_custom_call" | custom-call | tf_op jit(solution)/shard_map/pallas_call | solution.py:291
  169.9 0.0 collective-permute-done.11.theirs_ref
  169.9 0.0 copy-start.1
  169.9 3.1 %shard_map.74 = (bf16[256,3072]{1,0:T(8,128)(2,1)}, f32[16,8,128]{2,1,0:T(8,128)S(1)}) custom-call(s32[5]{0:T(128)S(1)} %stack.23.core_ref.info_ref, f32[256,1536]{1,0:T(8,128)S(1)} %shard_map.73.mine_ref, f32[256,1536]{1,0:T(8,128)S(1)} %collective-permute-done.11.theirs_ref, bf16[256,3072]{1,0:T(8,128)(2,1)S(1)} %bitcast.10, ...), custom_call_target="tpu_custom_call" | custom-call | tf_op jit(solution)/shard_map/pallas_call | solution.py:304
  173.0 24.7 %all_to_all.21.back_ref = f32[16,8,128]{2,1,0:T(8,128)S(1)} all-to-all(f32[16,8,128]{2,1,0:T(8,128)S(1)} %get-tuple-element.13), channel_id=1, replica_groups=mesh['zh'=2,'y'=8,'zl'=4,'x'=4,'c'=2] {'zh','y'}, dimensions={0} | all-to-all | bytes 131072 | tf_op jit(solution)/shard_map/all_to_all | solution.py:315
  197.7 0.8 shard_map.75
  (18 shorter events, 0.1 us)
Async XLA Ops:
  0.6 12.5 %copy-start.8 = (bf16[1,1536,128]{2,1,0:T(8,128)(2,1)S(1)}, bf16[1,1536,128]{2,1,0:T(8,128)(2,1)}, u32[]{:S(2)}) copy-start(bf16[1,1536,128]{2,1,0:T(8,128)(2,1)} %param.9) | copy-start | bytes 1179652
  0.6 13.8 %collective-permute-start.3 = (bf16[1,1536,128]{2,1,0:T(8,128)(2,1)}, bf16[1,1536,128]{2,1,0:T(8,128)(2,1)}, u32[]{:S(2)}, u32[]{:S(2)}) collective-permute-start(bf16[1,1536,128]{2,1,0:T(8,128)(2,1)} %param.9), channel_id=1, source_target_pairs={{8,0},{16,8},{24,16},{0,24},{9,1},{17,9},{25,17},{1,25},{10,2},{18... | collective-permute-start | bytes 1179656 | tf_op jit(solution)/shard_map/ppermute | solution.py:220
  9.3 6.2 %collective-permute-start = (bf16[144,2048]{1,0:T(8,128)(2,1)S(1)}, bf16[144,2048]{1,0:T(8,128)(2,1)S(1)}, u32[]{:S(2)}, u32[]{:S(2)}) collective-permute-start(bf16[144,2048]{1,0:T(8,128)(2,1)S(1)} %get-tuple-element.8), channel_id=1, source_target_pairs={{1,0},{0,1},{3,2},{2,3},{5,4},{4,5},{7,6},{6,7},{9,8},{8,9},{11,10... | collective-permute-start | bytes 1769480 | tf_op jit(solution)/shard_map/ppermute | solution.py:255
  11.2 14.7 %collective-permute-start.4 = (bf16[1,1536,128]{2,1,0:T(8,128)(2,1)}, bf16[1,1536,128]{2,1,0:T(8,128)(2,1)}, u32[]{:S(2)}, u32[]{:S(2)}) collective-permute-start(bf16[1,1536,128]{2,1,0:T(8,128)(2,1)} %param.9), channel_id=1, source_target_pairs={{24,0},{0,8},{8,16},{16,24},{25,1},{1,9},{9,17},{17,25},{26,2},{2,... | collective-permute-start | bytes 1179656 | tf_op jit(solution)/shard_map/ppermute | solution.py:220
  17.5 24.0 %all-to-all-start.2 = ((bf16[8,256,128]{2,1,0:T(8,128)(2,1)}), bf16[8,256,128]{2,1,0:T(8,128)(2,1)S(1)}, u32[]{:S(2)}, u32[]{:S(2)}) async-start(bf16[8,256,128]{2,1,0:T(8,128)(2,1)} %shard_map.71), calls=%async_computation.2 | async-start | bytes 1048576 | tf_op jit(solution)/shard_map/all_to_all | solution.py:267
  26.9 41.1 %copy-start.3 = (bf16[3,1536,128]{2,1,0:T(8,128)(2,1)}, bf16[3,1536,128]{2,1,0:T(8,128)(2,1)S(1)}, u32[]{:S(2)}) copy-start(bf16[3,1536,128]{2,1,0:T(8,128)(2,1)S(1)} %constant_dynamic-update-slice_fusion.refs_0_) | copy-start | bytes 3538948
  27.0 29.1 %collective-permute-start.5 = (bf16[3,1536,128]{2,1,0:T(8,128)(2,1)S(1)}, bf16[3,1536,128]{2,1,0:T(8,128)(2,1)}, u32[]{:S(2)}, u32[]{:S(2)}) collective-permute-start(bf16[3,1536,128]{2,1,0:T(8,128)(2,1)S(1)} %constant_dynamic-update-slice_fusion.refs_0_), channel_id=1, source_target_pairs={{2,0},{4,2},{6,4},{0,6},{3,1},{5,3},{7,5},{1,7},{10,8},{12,10},{14... | collective-permute-start | bytes 3538952 | tf_op jit(solution)/shard_map/ppermute | solution.py:220
  31.7 41.1 %collective-permute-start.6 = (bf16[3,1536,128]{2,1,0:T(8,128)(2,1)S(1)}, bf16[3,1536,128]{2,1,0:T(8,128)(2,1)}, u32[]{:S(2)}, u32[]{:S(2)}) collective-permute-start(bf16[3,1536,128]{2,1,0:T(8,128)(2,1)S(1)} %constant_dynamic-update-slice_fusion.refs_0_), channel_id=1, source_target_pairs={{6,0},{0,2},{2,4},{4,6},{7,1},{1,3},{3,5},{5,7},{14,8},{8,10},{10,... | collective-permute-start | bytes 3538952 | tf_op jit(solution)/shard_map/ppermute | solution.py:220
  41.5 0.8 copy-start.5
  42.3 62.3 %all-to-all-start = ((bf16[8,520,128]{2,1,0:T(8,128)(2,1)}), bf16[8,520,128]{2,1,0:T(8,128)(2,1)S(1)}, u32[]{:S(2)}, u32[]{:S(2)}) async-start(bf16[8,520,128]{2,1,0:T(8,128)(2,1)} %shard_map.69), calls=%async_computation | async-start | bytes 2129920 | tf_op jit(solution)/shard_map/all_to_all | solution.py:267
  45.9 21.0 %collective-permute-start.7 = (bf16[1,1536,128]{2,1,0:T(8,128)(2,1)}, bf16[1,1536,128]{2,1,0:T(8,128)(2,1)S(1)}, u32[]{:S(2)}, u32[]{:S(2)}) collective-permute-start(bf16[1,1536,128]{2,1,0:T(8,128)(2,1)} %param.9), channel_id=1, source_target_pairs={{16,0},{24,8},{0,16},{8,24},{17,1},{25,9},{1,17},{9,25},{18,2},{26... | collective-permute-start | bytes 1179656 | tf_op jit(solution)/shard_map/ppermute | solution.py:220
  66.8 16.8 %copy-start.2 = (bf16[1,1536,128]{2,1,0:T(8,128)(2,1)}, bf16[1,1536,128]{2,1,0:T(8,128)(2,1)S(1)}, u32[]{:S(2)}) copy-start(bf16[1,1536,128]{2,1,0:T(8,128)(2,1)S(1)} %collective-permute-done.7.refs_3_) | copy-start | bytes 1179652
  68.0 7.8 %copy-start.6 = (bf16[8,256,128]{2,1,0:T(8,128)(2,1)S(1)}, bf16[8,256,128]{2,1,0:T(8,128)(2,1)}, u32[]{:S(2)}) copy-start(bf16[8,256,128]{2,1,0:T(8,128)(2,1)} %copy-done.5) | copy-start | bytes 1572868
  68.0 39.0 %collective-permute-start.9 = (bf16[3,1536,128]{2,1,0:T(8,128)(2,1)}, bf16[3,1536,128]{2,1,0:T(8,128)(2,1)}, u32[]{:S(2)}, u32[]{:S(2)}) collective-permute-start(bf16[3,1536,128]{2,1,0:T(8,128)(2,1)} %pad_maximum_fusion), channel_id=1, source_target_pairs={{2,0},{4,2},{6,4},{0,6},{3,1},{5,3},{7,5},{1,7},{10,8},{12,10},{14... | collective-permute-start | bytes 3538952 | tf_op jit(solution)/shard_map/ppermute | solution.py:220
  73.9 30.7 %collective-permute-start.10 = (bf16[2,1536,128]{2,1,0:T(8,128)(2,1)S(1)}, bf16[2,1536,128]{2,1,0:T(8,128)(2,1)S(1)}, u32[]{:S(2)}, u32[]{:S(2)}) collective-permute-start(bf16[2,1536,128]{2,1,0:T(8,128)(2,1)S(1)} %pad_maximum_fusion.1), channel_id=1, source_target_pairs={{6,0},{0,2},{2,4},{4,6},{7,1},{1,3},{3,5},{5,7},{14,8},{8,10},{10,... | collective-permute-start | bytes 2359304 | tf_op jit(solution)/shard_map/ppermute | solution.py:220
  75.9 27.9 %collective-permute-start.2 = (bf16[8,256,128]{2,1,0:T(8,128)(2,1)S(1)}, bf16[8,256,128]{2,1,0:T(8,128)(2,1)S(1)}, u32[]{:S(2)}, u32[]{:S(2)}) collective-permute-start(bf16[8,256,128]{2,1,0:T(8,128)(2,1)S(1)} %copy-done.6), channel_id=1, source_target_pairs={{256,0},{0,256},{257,1},{1,257},{258,2},{2,258},{259,3},{3,259},{2... | collective-permute-start | bytes 1572872 | tf_op jit(solution)/shard_map/ppermute | solution.py:270
  83.7 20.1 %collective-permute-start.8 = (bf16[1,1536,128]{2,1,0:T(8,128)(2,1)S(1)}, bf16[1,1536,128]{2,1,0:T(8,128)(2,1)S(1)}, u32[]{:S(2)}, u32[]{:S(2)}) collective-permute-start(bf16[1,1536,128]{2,1,0:T(8,128)(2,1)S(1)} %collective-permute-done.7.refs_3_), channel_id=1, source_target_pairs={{4,0},{6,2},{0,4},{2,6},{5,1},{7,3},{1,5},{3,7},{12,8},{14,10},{8,... | collective-permute-start | bytes 1179656 | tf_op jit(solution)/shard_map/ppermute | solution.py:220
  103.8 0.7 copy-start.7
  104.6 2.3 %copy-start.4 = (bf16[2,1536,128]{2,1,0:T(8,128)(2,1)}, bf16[2,1536,128]{2,1,0:T(8,128)(2,1)S(1)}, u32[]{:S(2)}) copy-start(bf16[2,1536,128]{2,1,0:T(8,128)(2,1)S(1)} %collective-permute-done.10.refs_6_) | copy-start | bytes 2359300
  112.0 57.9 %collective-permute-start.11 = (f32[256,1536]{1,0:T(8,128)S(1)}, f32[256,1536]{1,0:T(8,128)S(1)}, u32[]{:S(2)}, u32[]{:S(2)}) collective-permute-start(f32[256,1536]{1,0:T(8,128)S(1)} %get-tuple-element.11), channel_id=1, source_target_pairs={{1,0},{0,1},{3,2},{2,3},{5,4},{4,5},{7,6},{6,7},{9,8},{8,9},{11,10... | collective-permute-start | bytes 4718600 | tf_op jit(solution)/shard_map/ppermute | solution.py:290
  140.2 26.4 %collective-permute-start.1 = (bf16[8,264,128]{2,1,0:T(8,128)(2,1)S(1)}, bf16[8,264,128]{2,1,0:T(8,128)(2,1)S(1)}, u32[]{:S(2)}, u32[]{:S(2)}) collective-permute-start(bf16[8,264,128]{2,1,0:T(8,128)(2,1)S(1)} %all_to_all.20), channel_id=1, source_target_pairs={{256,0},{0,256},{257,1},{1,257},{258,2},{2,258},{259,3},{3,259},{2... | collective-permute-start | bytes 1622024 | tf_op jit(solution)/shard_map/ppermute | solution.py:270
  166.6 3.3 %copy-start = (bf16[1,1,256,3072]{3,2,1,0:T(8,128)(2,1)S(1)}, bf16[1,1,256,3072]{3,2,1,0:T(8,128)(2,1)}, u32[]{:S(2)}) copy-start(bf16[1,1,256,3072]{3,2,1,0:T(8,128)(2,1)} %param.8) | copy-start | bytes 4718596
  169.9 27.8 %copy-start.1 = (s32[128,8]{0,1:T(8,128)S(1)}, s32[128,8]{0,1:T(8,128)}, u32[]{:S(2)}) copy-start(s32[128,8]{0,1:T(8,128)} %param.6) | copy-start | bytes 12292

commit v2 on v1

--- a/solution.py
+++ b/solution.py
@@ -222,14 +222,15 @@
 
 def gather_weights(block):
     z1, z3, z2 = (permute(block, "zl", r) for r in (1, 3, 2))
+    a2 = permute(block, "x", 2)
     trio = jnp.concatenate([block, z1, z3], axis=0)
     g1, g3 = permute(trio, "x", 1), permute(trio, "x", 3)
-    e2 = permute(z2, "x", 2)
-    f1 = permute(jnp.concatenate([g1[:2], z2], axis=0), "x", 1)
-    f3 = permute(jnp.concatenate([g3[2:], z2], axis=0), "x", 3)
+    h1, h3, e2 = permute(z2, "x", 1), permute(z2, "x", 3), permute(z2, "x", 2)
+    from_up, from_down = g1[1:2], g3[2:]
+    f1, f3 = permute(from_up, "x", 1), permute(from_down, "x", 3)
     groups = [(a, [(dz, dx) for dz in (0, 1, 3)]) for a, dx in ((trio, 0), (g1, 1), (g3, 3))]
-    groups += [(z2, [(2, 0)]), (e2, [(2, 2)])]
-    return groups + [(f1, [(0, 2), (1, 2), (2, 1)]), (f3, [(3, 2), (2, 3)])]
+    groups += [(a, [(2, dx)]) for a, dx in ((z2, 0), (h1, 1), (h3, 3), (e2, 2))]
+    return groups + [(a2, [(0, 2)]), (f1, [(1, 2)]), (f3, [(3, 2)])]
 
 
 def step(grad_out, routes, gate, saved, w_down):

time: 199 us -> 203 us (1.020)
  the two profiles are of different devices: /device:TPU:64 before, /device:TPU:128 now
where the time goes in v2:
time: 203 us; the launch traced here: 202 us
  starting transfers between devices  67.6 us (33%)
  waiting for transfers between devices  65.1 us (32%)
  blocking collectives  44.1 us (22%)
  Pallas kernels  19.1 us (9%)
  local copies, waits for them, and re-layouts  5.26 us (3%)
    ppermute x11, starting transfers between devices, permute(): return lax.ppermute(array, axis, ring(4, shift))  35.2 us
    ppermute x11, waiting for transfers between devices, permute(): return lax.ppermute(array, axis, ring(4, shift))  31.7 us
    all_to_all x1, blocking collectives, along_y(): return lax.all_to_all(array, 'y', split_axis=0, concat_axis=0, tiled=True)  25.2 us
    ppermute x2, waiting for transfers between devices, across(): return lax.ppermute(array, 'zh', ring(2, 1))  24 us
    all_to_all x1, blocking collectives, step(): back = lax.all_to_all(score, EP, split_axis=0, concat_axis=0, tiled=True)  18.9 us
    ppermute x2, starting transfers between devices, across(): return lax.ppermute(array, 'zh', ring(2, 1))  17.9 us
    all_to_all x2, starting transfers between devices, along_y(): return lax.all_to_all(array, 'y', split_axis=0, concat_axis=0, tiled=True)  10.7 us
    all_to_all x2, waiting for transfers between devices, along_y(): return lax.all_to_all(array, 'y', split_axis=0, concat_axis=0, tiled=True)  7.45 us
  transfers between devices with their start and end apart: 17, of which 10 were waited for; matrix products, arithmetic and copies ran while one was open for 2% of the time, Pallas kernels for 3%

profile of v2, /device:TPU:128, one launch (start us, length us, event | category | flops | bytes accessed | tf_op | source)
XLA Modules:
  0.0 202.1 jit_solution(8953216134062319653)
XLA Ops:
  0.6 0.1 stack.23.core_ref.info_ref
  0.7 1.5 shard_map.68
  2.2 1.9 collective-permute-start
  4.2 2.0 collective-permute-done.got_ref
  6.1 1.9 shard_map.71
  8.1 7.1 %all-to-all-start.2 = ((bf16[8,256,128]{2,1,0:T(8,128)(2,1)}), bf16[8,256,128]{2,1,0:T(8,128)(2,1)S(1)}, u32[]{:S(2)}, u32[]{:S(2)}) async-start(bf16[8,256,128]{2,1,0:T(8,128)(2,1)} %shard_map.71), calls=%async_computation.2 | async-start | bytes 1048576 | tf_op jit(solution)/shard_map/all_to_all | solution.py:268
  15.2 1.9 collective-permute-start.3
  17.1 4.3 %collective-permute-start.4 = (bf16[1,1536,128]{2,1,0:T(8,128)(2,1)}, bf16[1,1536,128]{2,1,0:T(8,128)(2,1)S(1)}, u32[]{:S(2)}, u32[]{:S(2)}) collective-permute-start(bf16[1,1536,128]{2,1,0:T(8,128)(2,1)} %param.9), channel_id=1, source_target_pairs={{24,0},{0,8},{8,16},{16,24},{25,1},{1,9},{9,17},{17,25},{26,2},{2,... | collective-permute-start | bytes 1179656 | tf_op jit(solution)/shard_map/ppermute | solution.py:220
  21.4 1.8 constant_dynamic-update-slice_fusion.2
  23.2 2.4 %shard_map.69 = bf16[8,520,128]{2,1,0:T(8,128)(2,1)} custom-call(s32[5]{0:T(128)S(1)} %stack.23.core_ref.info_ref, bf16[144,2048]{1,0:T(8,128)(2,1)S(1)} %collective-permute-done.got_ref, bf16[128,2048]{1,0:T(8,128)(2,1)S(1)} %get-tuple-element.9.keep_ref, s32[8,128]{1,0:T(8,128)} %bitcast.13, bf16[8,128]{1,0:T(8,128)(2,1)} %bitcast.17), custom_call_target="tpu_custom_call" | custom-call | tf_op jit(solution)/shard_map/pallas_call | solution.py:262
  25.5 7.5 %all-to-all-done.2 = bf16[8,256,128]{2,1,0:T(8,128)(2,1)S(1)} async-done(((bf16[8,256,128]{2,1,0:T(8,128)(2,1)}), bf16[8,256,128]{2,1,0:T(8,128)(2,1)S(1)}, u32[]{:S(2)}, u32[]{:S(2)}) %all-to-all-start.2) | async-done | bytes 524320 | tf_op jit(solution)/shard_map/all_to_all | solution.py:268
  33.0 3.6 %all-to-all-start = ((bf16[8,520,128]{2,1,0:T(8,128)(2,1)}), bf16[8,520,128]{2,1,0:T(8,128)(2,1)S(1)}, u32[]{:S(2)}, u32[]{:S(2)}) async-start(bf16[8,520,128]{2,1,0:T(8,128)(2,1)} %shard_map.69), calls=%async_computation | async-start | bytes 2129920 | tf_op jit(solution)/shard_map/all_to_all | solution.py:268
  36.5 0.0 collective-permute-done.3
  36.5 1.8 constant_dynamic-update-slice_fusion.1
  38.3 0.2 collective-permute-done.4
  38.5 0.8 constant_dynamic-update-slice_fusion.refs_0_
  39.3 4.7 %collective-permute-start.5 = (bf16[3,1536,128]{2,1,0:T(8,128)(2,1)}, bf16[3,1536,128]{2,1,0:T(8,128)(2,1)S(1)}, u32[]{:S(2)}, u32[]{:S(2)}) collective-permute-start(bf16[3,1536,128]{2,1,0:T(8,128)(2,1)} %constant_dynamic-update-slice_fusion.refs_0_), channel_id=1, source_target_pairs={{2,0},{4,2},{6,4},{0,6},{3,1},{5,3},{7,5},{1,7},{10,8},{12,10},{14... | collective-permute-start | bytes 3538952 | tf_op jit(solution)/shard_map/ppermute | solution.py:220
  43.9 1.9 collective-permute-start.6
  45.9 3.0 %collective-permute-start.7 = (bf16[1,1536,128]{2,1,0:T(8,128)(2,1)}, bf16[1,1536,128]{2,1,0:T(8,128)(2,1)S(1)}, u32[]{:S(2)}, u32[]{:S(2)}) collective-permute-start(bf16[1,1536,128]{2,1,0:T(8,128)(2,1)} %param.9), channel_id=1, source_target_pairs={{16,0},{24,8},{0,16},{8,24},{17,1},{25,9},{1,17},{9,25},{18,2},{26... | collective-permute-start | bytes 1179656 | tf_op jit(solution)/shard_map/ppermute | solution.py:220
  48.9 4.2 %collective-permute-start.11 = (bf16[1,1536,128]{2,1,0:T(8,128)(2,1)}, bf16[1,1536,128]{2,1,0:T(8,128)(2,1)S(1)}, u32[]{:S(2)}, u32[]{:S(2)}) collective-permute-start(bf16[1,1536,128]{2,1,0:T(8,128)(2,1)} %param.9), channel_id=1, source_target_pairs={{4,0},{6,2},{0,4},{2,6},{5,1},{7,3},{1,5},{3,7},{12,8},{14,10},{8,... | collective-permute-start | bytes 1179656 | tf_op jit(solution)/shard_map/ppermute | solution.py:220
  53.0 12.1 %collective-permute-done.7.refs_3_ = bf16[1,1536,128]{2,1,0:T(8,128)(2,1)S(1)} collective-permute-done((bf16[1,1536,128]{2,1,0:T(8,128)(2,1)}, bf16[1,1536,128]{2,1,0:T(8,128)(2,1)S(1)}, u32[]{:S(2)}, u32[]{:S(2)}) %collective-permute-start.7) | collective-permute-done | bytes 393248 | tf_op jit(solution)/shard_map/ppermute | solution.py:220
  65.1 4.8 %collective-permute-start.8 = (bf16[1,1536,128]{2,1,0:T(8,128)(2,1)S(1)}, bf16[1,1536,128]{2,1,0:T(8,128)(2,1)S(1)}, u32[]{:S(2)}, u32[]{:S(2)}) collective-permute-start(bf16[1,1536,128]{2,1,0:T(8,128)(2,1)S(1)} %collective-permute-done.7.refs_3_), channel_id=1, source_target_pairs={{2,0},{4,2},{6,4},{0,6},{3,1},{5,3},{7,5},{1,7},{10,8},{12,10},{14... | collective-permute-start | bytes 1179656 | tf_op jit(solution)/shard_map/ppermute | solution.py:220
  70.0 9.1 %collective-permute-start.2 = (bf16[8,256,128]{2,1,0:T(8,128)(2,1)S(1)}, bf16[8,256,128]{2,1,0:T(8,128)(2,1)S(1)}, u32[]{:S(2)}, u32[]{:S(2)}) collective-permute-start(bf16[8,256,128]{2,1,0:T(8,128)(2,1)S(1)} %all-to-all-done.2), channel_id=1, source_target_pairs={{256,0},{0,256},{257,1},{1,257},{258,2},{2,258},{259,3},{3,259},{2... | collective-permute-start | bytes 1572872 | tf_op jit(solution)/shard_map/ppermute | solution.py:271
  79.1 1.9 collective-permute-start.9
  81.1 2.2 %collective-permute-done.6.refs_2_ = bf16[3,1536,128]{2,1,0:T(8,128)(2,1)S(1)} collective-permute-done((bf16[3,1536,128]{2,1,0:T(8,128)(2,1)}, bf16[3,1536,128]{2,1,0:T(8,128)(2,1)S(1)}, u32[]{:S(2)}, u32[]{:S(2)}) %collective-permute-start.6) | collective-permute-done | bytes 1179680 | tf_op jit(solution)/shard_map/ppermute | solution.py:220
  83.3 4.7 %collective-permute-start.10 = (bf16[1,1536,128]{2,1,0:T(8,128)(2,1)S(1)}, bf16[1,1536,128]{2,1,0:T(8,128)(2,1)S(1)}, u32[]{:S(2)}, u32[]{:S(2)}) collective-permute-start(bf16[1,1536,128]{2,1,0:T(8,128)(2,1)S(1)} %collective-permute-done.7.refs_3_), channel_id=1, source_target_pairs={{4,0},{6,2},{0,4},{2,6},{5,1},{7,3},{1,5},{3,7},{12,8},{14,10},{8,... | collective-permute-start | bytes 1179656 | tf_op jit(solution)/shard_map/ppermute | solution.py:220
  88.0 0.0 collective-permute-done.11.refs_7_
  88.0 1.9 collective-permute-start.12
  89.9 4.8 %collective-permute-done.8.refs_4_ = bf16[1,1536,128]{2,1,0:T(8,128)(2,1)S(1)} collective-permute-done((bf16[1,1536,128]{2,1,0:T(8,128)(2,1)S(1)}, bf16[1,1536,128]{2,1,0:T(8,128)(2,1)S(1)}, u32[]{:S(2)}, u32[]{:S(2)}) %collective-permute-start.8) | collective-permute-done | bytes 393248 | tf_op jit(solution)/shard_map/ppermute | solution.py:220
  94.8 1.9 collective-permute-start.13
  96.7 0.0 collective-permute-done.9.refs_5_
  96.7 5.8 %collective-permute-done.10.refs_6_ = bf16[1,1536,128]{2,1,0:T(8,128)(2,1)S(1)} collective-permute-done((bf16[1,1536,128]{2,1,0:T(8,128)(2,1)S(1)}, bf16[1,1536,128]{2,1,0:T(8,128)(2,1)S(1)}, u32[]{:S(2)}, u32[]{:S(2)}) %collective-permute-start.10) | collective-permute-done | bytes 393248 | tf_op jit(solution)/shard_map/ppermute | solution.py:220
  102.5 0.7 collective-permute-done.12.refs_8_
  103.2 6.0 %collective-permute-done.13.refs_9_ = bf16[1,1536,128]{2,1,0:T(8,128)(2,1)S(1)} collective-permute-done((bf16[1,1536,128]{2,1,0:T(8,128)(2,1)S(1)}, bf16[1,1536,128]{2,1,0:T(8,128)(2,1)S(1)}, u32[]{:S(2)}, u32[]{:S(2)}) %collective-permute-start.13) | collective-permute-done | bytes 393248 | tf_op jit(solution)/shard_map/ppermute | solution.py:220
  109.3 0.8 copy-done.10
  110.0 0.0 collective-permute-done.2.cross_ref
  110.0 5.1 %shard_map.72 = (f32[256,1536]{1,0:T(8,128)S(1)}, bf16[1536,2048]{1,0:T(8,128)(2,1)S(1)}) custom-call(s32[5]{0:T(128)S(1)} %stack.23.core_ref.info_ref, bf16[8,520,128]{2,1,0:T(8,128)(2,1)S(1)} %all-to-all-done.stay_ref, bf16[8,256,128]{2,1,0:T(8,128)(2,1)S(1)} %collective-permute-done.2.cross_ref, ...), custom_call_target="tpu_custom_call" | custom-call | tf_op jit(solution)/shard_map/pallas_call | solution.py:282
  115.1 1.9 collective-permute-start.14
  117.0 1.1 shard_map.70
  118.2 25.2 %all_to_all.20 = bf16[8,264,128]{2,1,0:T(8,128)(2,1)S(1)} all-to-all(bf16[8,264,128]{2,1,0:T(8,128)(2,1)S(1)} %shard_map.70), channel_id=1, replica_groups=mesh['zh'=2,'y'=8,'zl'=4,'x'=4,'c'=2] {'y'}, dimensions={0} | all-to-all | bytes 1081344 | tf_op jit(solution)/shard_map/all_to_all | solution.py:268
  143.4 8.8 %collective-permute-start.1 = (bf16[8,264,128]{2,1,0:T(8,128)(2,1)S(1)}, bf16[8,264,128]{2,1,0:T(8,128)(2,1)S(1)}, u32[]{:S(2)}, u32[]{:S(2)}) collective-permute-start(bf16[8,264,128]{2,1,0:T(8,128)(2,1)S(1)} %all_to_all.20), channel_id=1, source_target_pairs={{256,0},{0,256},{257,1},{1,257},{258,2},{2,258},{259,3},{3,259},{2... | collective-permute-start | bytes 1622024 | tf_op jit(solution)/shard_map/ppermute | solution.py:271
  152.1 24.0 %collective-permute-done.1.cross_ref = bf16[8,264,128]{2,1,0:T(8,128)(2,1)S(1)} collective-permute-done((bf16[8,264,128]{2,1,0:T(8,128)(2,1)S(1)}, bf16[8,264,128]{2,1,0:T(8,128)(2,1)S(1)}, u32[]{:S(2)}, u32[]{:S(2)}) %collective-permute-start.1) | collective-permute-done | bytes 540704 | tf_op jit(solution)/shard_map/ppermute | solution.py:271
  176.1 3.3 %shard_map.73.mine_ref = f32[256,1536]{1,0:T(8,128)S(1)} custom-call(s32[5]{0:T(128)S(1)} %stack.23.core_ref.info_ref, bf16[8,520,128]{2,1,0:T(8,128)(2,1)S(1)} %all-to-all-done.stay_ref, bf16[8,264,128]{2,1,0:T(8,128)(2,1)S(1)} %collective-permute-done.1.cross_ref, bf16[1536,2048]{1,0:T(8,128)(2,1)S(1)} %get-tuple-element.10.whole_ref), custom_call_target="tpu_custom_call" | custom-call | tf_op jit(solution)/shard_map/pallas_call | solution.py:292
  179.4 0.0 collective-permute-done.14.theirs_ref
  179.4 0.0 copy-start.1
  179.4 3.1 %shard_map.74 = (bf16[256,3072]{1,0:T(8,128)(2,1)}, f32[16,8,128]{2,1,0:T(8,128)S(1)}) custom-call(s32[5]{0:T(128)S(1)} %stack.23.core_ref.info_ref, f32[256,1536]{1,0:T(8,128)S(1)} %shard_map.73.mine_ref, f32[256,1536]{1,0:T(8,128)S(1)} %collective-permute-done.14.theirs_ref, bf16[256,3072]{1,0:T(8,128)(2,1)S(1)} %bitcast.10, ...), custom_call_target="tpu_custom_call" | custom-call | tf_op jit(solution)/shard_map/pallas_call | solution.py:305
  182.5 18.9 %all_to_all.21.back_ref = f32[16,8,128]{2,1,0:T(8,128)S(1)} all-to-all(f32[16,8,128]{2,1,0:T(8,128)S(1)} %get-tuple-element.13), channel_id=1, replica_groups=mesh['zh'=2,'y'=8,'zl'=4,'x'=4,'c'=2] {'zh','y'}, dimensions={0} | all-to-all | bytes 131072 | tf_op jit(solution)/shard_map/all_to_all | solution.py:316
  201.3 0.8 shard_map.75
  (26 shorter events, 0.1 us)
Async XLA Ops:
  2.2 3.9 %collective-permute-start = (bf16[144,2048]{1,0:T(8,128)(2,1)S(1)}, bf16[144,2048]{1,0:T(8,128)(2,1)S(1)}, u32[]{:S(2)}, u32[]{:S(2)}) collective-permute-start(bf16[144,2048]{1,0:T(8,128)(2,1)S(1)} %get-tuple-element.8), channel_id=1, source_target_pairs={{1,0},{0,1},{3,2},{2,3},{5,4},{4,5},{7,6},{6,7},{9,8},{8,9},{11,10... | collective-permute-start | bytes 1769480 | tf_op jit(solution)/shard_map/ppermute | solution.py:256
  8.1 24.9 %all-to-all-start.2 = ((bf16[8,256,128]{2,1,0:T(8,128)(2,1)}), bf16[8,256,128]{2,1,0:T(8,128)(2,1)S(1)}, u32[]{:S(2)}, u32[]{:S(2)}) async-start(bf16[8,256,128]{2,1,0:T(8,128)(2,1)} %shard_map.71), calls=%async_computation.2 | async-start | bytes 1048576 | tf_op jit(solution)/shard_map/all_to_all | solution.py:268
  15.2 21.4 %collective-permute-start.3 = (bf16[1,1536,128]{2,1,0:T(8,128)(2,1)}, bf16[1,1536,128]{2,1,0:T(8,128)(2,1)}, u32[]{:S(2)}, u32[]{:S(2)}) collective-permute-start(bf16[1,1536,128]{2,1,0:T(8,128)(2,1)} %param.9), channel_id=1, source_target_pairs={{8,0},{16,8},{24,16},{0,24},{9,1},{17,9},{25,17},{1,25},{10,2},{18... | collective-permute-start | bytes 1179656 | tf_op jit(solution)/shard_map/ppermute | solution.py:220
  17.1 21.4 %collective-permute-start.4 = (bf16[1,1536,128]{2,1,0:T(8,128)(2,1)}, bf16[1,1536,128]{2,1,0:T(8,128)(2,1)S(1)}, u32[]{:S(2)}, u32[]{:S(2)}) collective-permute-start(bf16[1,1536,128]{2,1,0:T(8,128)(2,1)} %param.9), channel_id=1, source_target_pairs={{24,0},{0,8},{8,16},{16,24},{25,1},{1,9},{9,17},{17,25},{26,2},{2,... | collective-permute-start | bytes 1179656 | tf_op jit(solution)/shard_map/ppermute | solution.py:220
  33.0 77.1 %all-to-all-start = ((bf16[8,520,128]{2,1,0:T(8,128)(2,1)}), bf16[8,520,128]{2,1,0:T(8,128)(2,1)S(1)}, u32[]{:S(2)}, u32[]{:S(2)}) async-start(bf16[8,520,128]{2,1,0:T(8,128)(2,1)} %shard_map.69), calls=%async_computation | async-start | bytes 2129920 | tf_op jit(solution)/shard_map/all_to_all | solution.py:268
  39.3 39.8 %collective-permute-start.5 = (bf16[3,1536,128]{2,1,0:T(8,128)(2,1)}, bf16[3,1536,128]{2,1,0:T(8,128)(2,1)S(1)}, u32[]{:S(2)}, u32[]{:S(2)}) collective-permute-start(bf16[3,1536,128]{2,1,0:T(8,128)(2,1)} %constant_dynamic-update-slice_fusion.refs_0_), channel_id=1, source_target_pairs={{2,0},{4,2},{6,4},{0,6},{3,1},{5,3},{7,5},{1,7},{10,8},{12,10},{14... | collective-permute-start | bytes 3538952 | tf_op jit(solution)/shard_map/ppermute | solution.py:220
  43.9 39.3 %collective-permute-start.6 = (bf16[3,1536,128]{2,1,0:T(8,128)(2,1)}, bf16[3,1536,128]{2,1,0:T(8,128)(2,1)S(1)}, u32[]{:S(2)}, u32[]{:S(2)}) collective-permute-start(bf16[3,1536,128]{2,1,0:T(8,128)(2,1)} %constant_dynamic-update-slice_fusion.refs_0_), channel_id=1, source_target_pairs={{6,0},{0,2},{2,4},{4,6},{7,1},{1,3},{3,5},{5,7},{14,8},{8,10},{10,... | collective-permute-start | bytes 3538952 | tf_op jit(solution)/shard_map/ppermute | solution.py:220
  45.9 19.2 %collective-permute-start.7 = (bf16[1,1536,128]{2,1,0:T(8,128)(2,1)}, bf16[1,1536,128]{2,1,0:T(8,128)(2,1)S(1)}, u32[]{:S(2)}, u32[]{:S(2)}) collective-permute-start(bf16[1,1536,128]{2,1,0:T(8,128)(2,1)} %param.9), channel_id=1, source_target_pairs={{16,0},{24,8},{0,16},{8,24},{17,1},{25,9},{1,17},{9,25},{18,2},{26... | collective-permute-start | bytes 1179656 | tf_op jit(solution)/shard_map/ppermute | solution.py:220
  48.9 39.1 %collective-permute-start.11 = (bf16[1,1536,128]{2,1,0:T(8,128)(2,1)}, bf16[1,1536,128]{2,1,0:T(8,128)(2,1)S(1)}, u32[]{:S(2)}, u32[]{:S(2)}) collective-permute-start(bf16[1,1536,128]{2,1,0:T(8,128)(2,1)} %param.9), channel_id=1, source_target_pairs={{4,0},{6,2},{0,4},{2,6},{5,1},{7,3},{1,5},{3,7},{12,8},{14,10},{8,... | collective-permute-start | bytes 1179656 | tf_op jit(solution)/shard_map/ppermute | solution.py:220
  65.1 44.1 %copy-start.4 = (bf16[1,1536,128]{2,1,0:T(8,128)(2,1)}, bf16[1,1536,128]{2,1,0:T(8,128)(2,1)S(1)}, u32[]{:S(2)}) copy-start(bf16[1,1536,128]{2,1,0:T(8,128)(2,1)S(1)} %collective-permute-done.7.refs_3_) | copy-start | bytes 1179652
  65.1 29.6 %collective-permute-start.8 = (bf16[1,1536,128]{2,1,0:T(8,128)(2,1)S(1)}, bf16[1,1536,128]{2,1,0:T(8,128)(2,1)S(1)}, u32[]{:S(2)}, u32[]{:S(2)}) collective-permute-start(bf16[1,1536,128]{2,1,0:T(8,128)(2,1)S(1)} %collective-permute-done.7.refs_3_), channel_id=1, source_target_pairs={{2,0},{4,2},{6,4},{0,6},{3,1},{5,3},{7,5},{1,7},{10,8},{12,10},{14... | collective-permute-start | bytes 1179656 | tf_op jit(solution)/shard_map/ppermute | solution.py:220
  70.0 40.1 %collective-permute-start.2 = (bf16[8,256,128]{2,1,0:T(8,128)(2,1)S(1)}, bf16[8,256,128]{2,1,0:T(8,128)(2,1)S(1)}, u32[]{:S(2)}, u32[]{:S(2)}) collective-permute-start(bf16[8,256,128]{2,1,0:T(8,128)(2,1)S(1)} %all-to-all-done.2), channel_id=1, source_target_pairs={{256,0},{0,256},{257,1},{1,257},{258,2},{2,258},{259,3},{3,259},{2... | collective-permute-start | bytes 1572872 | tf_op jit(solution)/shard_map/ppermute | solution.py:271
  79.1 30.1 %copy-start.2 = (bf16[3,1536,128]{2,1,0:T(8,128)(2,1)}, bf16[3,1536,128]{2,1,0:T(8,128)(2,1)S(1)}, u32[]{:S(2)}) copy-start(bf16[3,1536,128]{2,1,0:T(8,128)(2,1)S(1)} %collective-permute-done.5.refs_1_) | copy-start | bytes 3538948
  79.1 17.5 %collective-permute-start.9 = (bf16[1,1536,128]{2,1,0:T(8,128)(2,1)S(1)}, bf16[1,1536,128]{2,1,0:T(8,128)(2,1)S(1)}, u32[]{:S(2)}, u32[]{:S(2)}) collective-permute-start(bf16[1,1536,128]{2,1,0:T(8,128)(2,1)S(1)} %collective-permute-done.7.refs_3_), channel_id=1, source_target_pairs={{6,0},{0,2},{2,4},{4,6},{7,1},{1,3},{3,5},{5,7},{14,8},{8,10},{10,... | collective-permute-start | bytes 1179656 | tf_op jit(solution)/shard_map/ppermute | solution.py:220
  83.3 26.0 %copy-start.3 = (bf16[3,1536,128]{2,1,0:T(8,128)(2,1)}, bf16[3,1536,128]{2,1,0:T(8,128)(2,1)S(1)}, u32[]{:S(2)}) copy-start(bf16[3,1536,128]{2,1,0:T(8,128)(2,1)S(1)} %collective-permute-done.6.refs_2_) | copy-start | bytes 3538948
  83.3 19.3 %collective-permute-start.10 = (bf16[1,1536,128]{2,1,0:T(8,128)(2,1)S(1)}, bf16[1,1536,128]{2,1,0:T(8,128)(2,1)S(1)}, u32[]{:S(2)}, u32[]{:S(2)}) collective-permute-start(bf16[1,1536,128]{2,1,0:T(8,128)(2,1)S(1)} %collective-permute-done.7.refs_3_), channel_id=1, source_target_pairs={{4,0},{6,2},{0,4},{2,6},{5,1},{7,3},{1,5},{3,7},{12,8},{14,10},{8,... | collective-permute-start | bytes 1179656 | tf_op jit(solution)/shard_map/ppermute | solution.py:220
  88.0 21.2 %copy-start.5 = (bf16[1,1536,128]{2,1,0:T(8,128)(2,1)}, bf16[1,1536,128]{2,1,0:T(8,128)(2,1)S(1)}, u32[]{:S(2)}) copy-start(bf16[1,1536,128]{2,1,0:T(8,128)(2,1)S(1)} %collective-permute-done.11.refs_7_) | copy-start | bytes 1179652
  88.0 15.2 %collective-permute-start.12 = (bf16[1,1536,128]{2,1,0:T(8,128)(2,1)S(1)}, bf16[1,1536,128]{2,1,0:T(8,128)(2,1)S(1)}, u32[]{:S(2)}, u32[]{:S(2)}) collective-permute-start(bf16[1,1536,128]{2,1,0:T(8,128)(2,1)S(1)} %slice.16), channel_id=1, source_target_pairs={{2,0},{4,2},{6,4},{0,6},{3,1},{5,3},{7,5},{1,7},{10,8},{12,10},{14... | collective-permute-start | bytes 1179656 | tf_op jit(solution)/shard_map/ppermute | solution.py:220
  94.8 14.5 %copy-start.6 = (bf16[1,1536,128]{2,1,0:T(8,128)(2,1)}, bf16[1,1536,128]{2,1,0:T(8,128)(2,1)S(1)}, u32[]{:S(2)}) copy-start(bf16[1,1536,128]{2,1,0:T(8,128)(2,1)S(1)} %collective-permute-done.8.refs_4_) | copy-start | bytes 1179652
  94.8 14.4 %collective-permute-start.13 = (bf16[1,1536,128]{2,1,0:T(8,128)(2,1)S(1)}, bf16[1,1536,128]{2,1,0:T(8,128)(2,1)S(1)}, u32[]{:S(2)}, u32[]{:S(2)}) collective-permute-start(bf16[1,1536,128]{2,1,0:T(8,128)(2,1)S(1)} %slice.17), channel_id=1, source_target_pairs={{6,0},{0,2},{2,4},{4,6},{7,1},{1,3},{3,5},{5,7},{14,8},{8,10},{10,... | collective-permute-start | bytes 1179656 | tf_op jit(solution)/shard_map/ppermute | solution.py:220
  96.7 12.5 %copy-start.7 = (bf16[1,1536,128]{2,1,0:T(8,128)(2,1)}, bf16[1,1536,128]{2,1,0:T(8,128)(2,1)S(1)}, u32[]{:S(2)}) copy-start(bf16[1,1536,128]{2,1,0:T(8,128)(2,1)S(1)} %collective-permute-done.9.refs_5_) | copy-start | bytes 1179652
  102.5 6.7 %copy-start.8 = (bf16[1,1536,128]{2,1,0:T(8,128)(2,1)}, bf16[1,1536,128]{2,1,0:T(8,128)(2,1)S(1)}, u32[]{:S(2)}) copy-start(bf16[1,1536,128]{2,1,0:T(8,128)(2,1)S(1)} %collective-permute-done.10.refs_6_) | copy-start | bytes 1179652
  103.2 6.0 %copy-start.9 = (bf16[1,1536,128]{2,1,0:T(8,128)(2,1)}, bf16[1,1536,128]{2,1,0:T(8,128)(2,1)S(1)}, u32[]{:S(2)}) copy-start(bf16[1,1536,128]{2,1,0:T(8,128)(2,1)S(1)} %collective-permute-done.12.refs_8_) | copy-start | bytes 1179652
  109.3 0.8 copy-start.10
  115.1 64.3 %collective-permute-start.14 = (f32[256,1536]{1,0:T(8,128)S(1)}, f32[256,1536]{1,0:T(8,128)S(1)}, u32[]{:S(2)}, u32[]{:S(2)}) collective-permute-start(f32[256,1536]{1,0:T(8,128)S(1)} %get-tuple-element.11), channel_id=1, source_target_pairs={{1,0},{0,1},{3,2},{2,3},{5,4},{4,5},{7,6},{6,7},{9,8},{8,9},{11,10... | collective-permute-start | bytes 4718600 | tf_op jit(solution)/shard_map/ppermute | solution.py:291
  143.4 32.7 %collective-permute-start.1 = (bf16[8,264,128]{2,1,0:T(8,128)(2,1)S(1)}, bf16[8,264,128]{2,1,0:T(8,128)(2,1)S(1)}, u32[]{:S(2)}, u32[]{:S(2)}) collective-permute-start(bf16[8,264,128]{2,1,0:T(8,128)(2,1)S(1)} %all_to_all.20), channel_id=1, source_target_pairs={{256,0},{0,256},{257,1},{1,257},{258,2},{2,258},{259,3},{3,259},{2... | collective-permute-start | bytes 1622024 | tf_op jit(solution)/shard_map/ppermute | solution.py:271
  176.1 3.3 %copy-start = (bf16[1,1,256,3072]{3,2,1,0:T(8,128)(2,1)S(1)}, bf16[1,1,256,3072]{3,2,1,0:T(8,128)(2,1)}, u32[]{:S(2)}) copy-start(bf16[1,1,256,3072]{3,2,1,0:T(8,128)(2,1)} %param.8) | copy-start | bytes 4718596
  179.4 21.9 %copy-start.1 = (s32[128,8]{0,1:T(8,128)S(1)}, s32[128,8]{0,1:T(8,128)}, u32[]{:S(2)}) copy-start(s32[128,8]{0,1:T(8,128)} %param.6) | copy-start | bytes 12292

commit v3 on v2

--- a/solution.py
+++ b/solution.py
@@ -155,8 +155,31 @@
     return ((i // 2) ^ info[STAY]) * 2 + i % 2
 
 
+def slopes_kernel(saved_ref, gate_slope_ref, up_slope_ref, hidden_ref):
+    units = hidden_ref.shape[1]
+    step = 256
+    for j in range(units // step):
+        cols = slice(j * step, (j + 1) * step)
+        a = saved_ref[:, cols].astype(F32)
+        u = saved_ref[:, units + j * step : units + (j + 1) * step].astype(F32)
+        sig = 1.0 / (1.0 + jnp.exp(-a))
+        silu = a * sig
+        hidden_ref[:, cols] = (silu * u).astype(BF16)
+        gate_slope_ref[:, cols] = u * sig * (1.0 + a * (1.0 - sig))
+        up_slope_ref[:, cols] = silu
+
+
 def finish_kernel(
-    info_ref, mine_ref, theirs_ref, saved_ref, stay_ref, cross_ref, out_ref, score_ref
+    info_ref,
+    mine_ref,
+    theirs_ref,
+    gate_slope_ref,
+    up_slope_ref,
+    hidden_ref,
+    stay_ref,
+    cross_ref,
+    out_ref,
+    score_ref,
 ):
     rows, units = mine_ref.shape
     number = piece(pl.program_id(0), info_ref)
@@ -170,15 +193,10 @@
         cols = slice(j * step, (j + 1) * step)
         up_cols = slice(units + j * step, units + (j + 1) * step)
         grad = mine_ref[:, cols] + theirs_ref[here, cols]
-        a = saved_ref[:, cols].astype(F32)
-        u = saved_ref[:, up_cols].astype(F32)
-        sig = 1.0 / (1.0 + jnp.exp(-a))
-        silu = a * sig
-        hidden = (silu * u).astype(BF16).astype(F32)
-        total += jnp.sum(grad * hidden, axis=1, keepdims=True)
+        total += jnp.sum(grad * hidden_ref[:, cols].astype(F32), axis=1, keepdims=True)
         scaled = grad * gate_in
-        out_ref[:, cols] = (scaled * u * sig * (1.0 + a * (1.0 - sig))).astype(BF16)
-        out_ref[:, up_cols] = (scaled * silu).astype(BF16)
+        out_ref[:, cols] = (scaled * gate_slope_ref[:, cols]).astype(BF16)
+        out_ref[:, up_cols] = (scaled * up_slope_ref[:, cols]).astype(BF16)
     score_ref[...] = jnp.broadcast_to(to_lanes(total, sources), score_ref.shape)
 
 
@@ -302,17 +320,28 @@
     tile = (sources // steps, 8, LANES)
     wide = pl.BlockSpec((rows, 2 * units), lambda i, info: (i, 0))
     gates = pl.BlockSpec(tile, lambda i, info: (i % 2, 0, 0))
+    narrow = pl.BlockSpec((rows, units), lambda i, info: (i, 0))
+    plain = pl.BlockSpec((rows, units), lambda i: (i, 0))
+    slopes = call(
+        slopes_kernel,
+        (product, product, jax.ShapeDtypeStruct((slots, units), BF16)),
+        [pl.BlockSpec((rows, 2 * units), lambda i: (i, 0))],
+        (plain,) * 3,
+        grid=(steps,),
+    )(saved[0, 0])
     grad_pre, score = call(
         finish_kernel,
         (
             jax.ShapeDtypeStruct((slots, 2 * units), BF16),
             jax.ShapeDtypeStruct((sources, 8, LANES), F32),
         ),
-        [pl.BlockSpec((rows, units), lambda i, info: (piece(i, info), 0)), VMEM, wide, gates, gates],
+        [pl.BlockSpec((rows, units), lambda i, info: (piece(i, info), 0)), VMEM]
+        + [narrow] * 3
+        + [gates, gates],
         (wide, pl.BlockSpec(tile, lambda i, info: (i, 0, 0))),
         grid=(steps,),
         prefetch=1,
-    )(info, mine, near(theirs), saved[0, 0], stay[:, 2 * height :, :], cross2[:, height:, :])
+    )(info, mine, near(theirs), *slopes, stay[:, 2 * height :, :], cross2[:, height:, :])
     back = lax.all_to_all(score, EP, split_axis=0, concat_axis=0, tiled=True)
     grad_gate = call(
         home_kernel, jax.ShapeDtypeStruct((routes.shape[1], tokens), F32), [VMEM, VMEM], VMEM

time: 203 us -> 203 us (level)
  transfers between devices with their start and end apart: 17 -> 17, of which waited for: 10 -> 10; matrix products, arithmetic and copies ran while one was open for 2% -> 2% of each run, Pallas kernels for 3% -> 4%
where the time goes in v3:
time: 203 us; the launch traced here: 202 us
  starting transfers between devices  67.7 us (33%)
  waiting for transfers between devices  64.3 us (32%)
  blocking collectives  44 us (22%)
  Pallas kernels  19.4 us (10%)
  local copies, waits for them, and re-layouts  5.25 us (3%)
    ppermute x11, starting transfers between devices, permute(): return lax.ppermute(array, axis, ring(4, shift))  35.2 us
    ppermute x11, waiting for transfers between devices, permute(): return lax.ppermute(array, axis, ring(4, shift))  31.7 us
    all_to_all x1, blocking collectives, along_y(): return lax.all_to_all(array, 'y', split_axis=0, concat_axis=0, tiled=True)  25.2 us
    ppermute x2, waiting for transfers between devices, across(): return lax.ppermute(array, 'zh', ring(2, 1))  23.1 us
    all_to_all x1, blocking collectives, step(): back = lax.all_to_all(score, EP, split_axis=0, concat_axis=0, tiled=True)  18.8 us
    ppermute x2, starting transfers between devices, across(): return lax.ppermute(array, 'zh', ring(2, 1))  17.9 us
    all_to_all x2, starting transfers between devices, along_y(): return lax.all_to_all(array, 'y', split_axis=0, concat_axis=0, tiled=True)  10.7 us
    all_to_all x2, waiting for transfers between devices, along_y(): return lax.all_to_all(array, 'y', split_axis=0, concat_axis=0, tiled=True)  7.45 us
  transfers between devices with their start and end apart: 17, of which 10 were waited for; matrix products, arithmetic and copies ran while one was open for 2% of the time, Pallas kernels for 4%

profile of v3, /device:TPU:128, one launch (start us, length us, event | category | flops | bytes accessed | tf_op | source)
XLA Modules:
  0.0 201.7 jit_solution(304403929326336896)
XLA Ops:
  0.6 0.1 stack.23.core_ref.info_ref
  0.7 1.5 shard_map.68
  2.2 1.9 collective-permute-start
  4.2 2.0 collective-permute-done.got_ref
  6.1 1.9 shard_map.71
  8.1 7.1 %all-to-all-start.2 = ((bf16[8,256,128]{2,1,0:T(8,128)(2,1)}), bf16[8,256,128]{2,1,0:T(8,128)(2,1)S(1)}, u32[]{:S(2)}, u32[]{:S(2)}) async-start(bf16[8,256,128]{2,1,0:T(8,128)(2,1)} %shard_map.71), calls=%async_computation.2 | async-start | bytes 1048576 | tf_op jit(solution)/shard_map/all_to_all | solution.py:286
  15.2 1.9 collective-permute-start.3
  17.1 4.3 %collective-permute-start.4 = (bf16[1,1536,128]{2,1,0:T(8,128)(2,1)}, bf16[1,1536,128]{2,1,0:T(8,128)(2,1)S(1)}, u32[]{:S(2)}, u32[]{:S(2)}) collective-permute-start(bf16[1,1536,128]{2,1,0:T(8,128)(2,1)} %param.9), channel_id=1, source_target_pairs={{24,0},{0,8},{8,16},{16,24},{25,1},{1,9},{9,17},{17,25},{26,2},{2,... | collective-permute-start | bytes 1179656 | tf_op jit(solution)/shard_map/ppermute | solution.py:238
  21.4 1.8 constant_dynamic-update-slice_fusion.2
  23.1 2.4 %shard_map.69 = bf16[8,520,128]{2,1,0:T(8,128)(2,1)} custom-call(s32[5]{0:T(128)S(1)} %stack.23.core_ref.info_ref, bf16[144,2048]{1,0:T(8,128)(2,1)S(1)} %collective-permute-done.got_ref, bf16[128,2048]{1,0:T(8,128)(2,1)S(1)} %get-tuple-element.12.keep_ref, s32[8,128]{1,0:T(8,128)} %bitcast.13, bf16[8,128]{1,0:T(8,128)(2,1)} %bitcast.17), custom_call_target="tpu_custom_call" | custom-call | tf_op jit(solution)/shard_map/pallas_call | solution.py:280
  25.5 7.4 %all-to-all-done.2 = bf16[8,256,128]{2,1,0:T(8,128)(2,1)S(1)} async-done(((bf16[8,256,128]{2,1,0:T(8,128)(2,1)}), bf16[8,256,128]{2,1,0:T(8,128)(2,1)S(1)}, u32[]{:S(2)}, u32[]{:S(2)}) %all-to-all-start.2) | async-done | bytes 524320 | tf_op jit(solution)/shard_map/all_to_all | solution.py:286
  32.9 3.6 %all-to-all-start = ((bf16[8,520,128]{2,1,0:T(8,128)(2,1)}), bf16[8,520,128]{2,1,0:T(8,128)(2,1)S(1)}, u32[]{:S(2)}, u32[]{:S(2)}) async-start(bf16[8,520,128]{2,1,0:T(8,128)(2,1)} %shard_map.69), calls=%async_computation | async-start | bytes 2129920 | tf_op jit(solution)/shard_map/all_to_all | solution.py:286
  36.5 0.0 collective-permute-done.3
  36.5 1.8 constant_dynamic-update-slice_fusion.1
  38.3 0.2 collective-permute-done.4
  38.5 0.8 constant_dynamic-update-slice_fusion.refs_0_
  39.3 4.7 %collective-permute-start.5 = (bf16[3,1536,128]{2,1,0:T(8,128)(2,1)}, bf16[3,1536,128]{2,1,0:T(8,128)(2,1)S(1)}, u32[]{:S(2)}, u32[]{:S(2)}) collective-permute-start(bf16[3,1536,128]{2,1,0:T(8,128)(2,1)} %constant_dynamic-update-slice_fusion.refs_0_), channel_id=1, source_target_pairs={{2,0},{4,2},{6,4},{0,6},{3,1},{5,3},{7,5},{1,7},{10,8},{12,10},{14... | collective-permute-start | bytes 3538952 | tf_op jit(solution)/shard_map/ppermute | solution.py:238
  43.9 1.9 collective-permute-start.6
  45.8 3.0 %collective-permute-start.7 = (bf16[1,1536,128]{2,1,0:T(8,128)(2,1)}, bf16[1,1536,128]{2,1,0:T(8,128)(2,1)S(1)}, u32[]{:S(2)}, u32[]{:S(2)}) collective-permute-start(bf16[1,1536,128]{2,1,0:T(8,128)(2,1)} %param.9), channel_id=1, source_target_pairs={{16,0},{24,8},{0,16},{8,24},{17,1},{25,9},{1,17},{9,25},{18,2},{26... | collective-permute-start | bytes 1179656 | tf_op jit(solution)/shard_map/ppermute | solution.py:238
  48.8 4.2 %collective-permute-start.11 = (bf16[1,1536,128]{2,1,0:T(8,128)(2,1)}, bf16[1,1536,128]{2,1,0:T(8,128)(2,1)S(1)}, u32[]{:S(2)}, u32[]{:S(2)}) collective-permute-start(bf16[1,1536,128]{2,1,0:T(8,128)(2,1)} %param.9), channel_id=1, source_target_pairs={{4,0},{6,2},{0,4},{2,6},{5,1},{7,3},{1,5},{3,7},{12,8},{14,10},{8,... | collective-permute-start | bytes 1179656 | tf_op jit(solution)/shard_map/ppermute | solution.py:238
  53.0 12.1 %collective-permute-done.7.refs_3_ = bf16[1,1536,128]{2,1,0:T(8,128)(2,1)S(1)} collective-permute-done((bf16[1,1536,128]{2,1,0:T(8,128)(2,1)}, bf16[1,1536,128]{2,1,0:T(8,128)(2,1)S(1)}, u32[]{:S(2)}, u32[]{:S(2)}) %collective-permute-start.7) | collective-permute-done | bytes 393248 | tf_op jit(solution)/shard_map/ppermute | solution.py:238
  65.1 4.8 %collective-permute-start.8 = (bf16[1,1536,128]{2,1,0:T(8,128)(2,1)S(1)}, bf16[1,1536,128]{2,1,0:T(8,128)(2,1)S(1)}, u32[]{:S(2)}, u32[]{:S(2)}) collective-permute-start(bf16[1,1536,128]{2,1,0:T(8,128)(2,1)S(1)} %collective-permute-done.7.refs_3_), channel_id=1, source_target_pairs={{2,0},{4,2},{6,4},{0,6},{3,1},{5,3},{7,5},{1,7},{10,8},{12,10},{14... | collective-permute-start | bytes 1179656 | tf_op jit(solution)/shard_map/ppermute | solution.py:238
  69.9 9.1 %collective-permute-start.2 = (bf16[8,256,128]{2,1,0:T(8,128)(2,1)S(1)}, bf16[8,256,128]{2,1,0:T(8,128)(2,1)S(1)}, u32[]{:S(2)}, u32[]{:S(2)}) collective-permute-start(bf16[8,256,128]{2,1,0:T(8,128)(2,1)S(1)} %all-to-all-done.2), channel_id=1, source_target_pairs={{256,0},{0,256},{257,1},{1,257},{258,2},{2,258},{259,3},{3,259},{2... | collective-permute-start | bytes 1572872 | tf_op jit(solution)/shard_map/ppermute | solution.py:289
  79.1 1.9 collective-permute-start.9
  81.1 2.2 %collective-permute-done.6.refs_2_ = bf16[3,1536,128]{2,1,0:T(8,128)(2,1)S(1)} collective-permute-done((bf16[3,1536,128]{2,1,0:T(8,128)(2,1)}, bf16[3,1536,128]{2,1,0:T(8,128)(2,1)S(1)}, u32[]{:S(2)}, u32[]{:S(2)}) %collective-permute-start.6) | collective-permute-done | bytes 1179680 | tf_op jit(solution)/shard_map/ppermute | solution.py:238
  83.2 4.7 %collective-permute-start.10 = (bf16[1,1536,128]{2,1,0:T(8,128)(2,1)S(1)}, bf16[1,1536,128]{2,1,0:T(8,128)(2,1)S(1)}, u32[]{:S(2)}, u32[]{:S(2)}) collective-permute-start(bf16[1,1536,128]{2,1,0:T(8,128)(2,1)S(1)} %collective-permute-done.7.refs_3_), channel_id=1, source_target_pairs={{4,0},{6,2},{0,4},{2,6},{5,1},{7,3},{1,5},{3,7},{12,8},{14,10},{8,... | collective-permute-start | bytes 1179656 | tf_op jit(solution)/shard_map/ppermute | solution.py:238
  88.0 0.0 collective-permute-done.11.refs_7_
  88.0 1.9 collective-permute-start.12
  89.9 4.8 %collective-permute-done.8.refs_4_ = bf16[1,1536,128]{2,1,0:T(8,128)(2,1)S(1)} collective-permute-done((bf16[1,1536,128]{2,1,0:T(8,128)(2,1)S(1)}, bf16[1,1536,128]{2,1,0:T(8,128)(2,1)S(1)}, u32[]{:S(2)}, u32[]{:S(2)}) %collective-permute-start.8) | collective-permute-done | bytes 393248 | tf_op jit(solution)/shard_map/ppermute | solution.py:238
  94.7 1.9 collective-permute-start.13
  96.7 5.8 %collective-permute-done.10.refs_6_ = bf16[1,1536,128]{2,1,0:T(8,128)(2,1)S(1)} collective-permute-done((bf16[1,1536,128]{2,1,0:T(8,128)(2,1)S(1)}, bf16[1,1536,128]{2,1,0:T(8,128)(2,1)S(1)}, u32[]{:S(2)}, u32[]{:S(2)}) %collective-permute-start.10) | collective-permute-done | bytes 393248 | tf_op jit(solution)/shard_map/ppermute | solution.py:238
  102.5 0.7 collective-permute-done.12.refs_8_
  103.2 6.0 %collective-permute-done.13.refs_9_ = bf16[1,1536,128]{2,1,0:T(8,128)(2,1)S(1)} collective-permute-done((bf16[1,1536,128]{2,1,0:T(8,128)(2,1)S(1)}, bf16[1,1536,128]{2,1,0:T(8,128)(2,1)S(1)}, u32[]{:S(2)}, u32[]{:S(2)}) %collective-permute-start.13) | collective-permute-done | bytes 393248 | tf_op jit(solution)/shard_map/ppermute | solution.py:238
  109.2 0.7 copy-done.10
  110.0 5.1 %shard_map.72 = (f32[256,1536]{1,0:T(8,128)S(1)}, bf16[1536,2048]{1,0:T(8,128)(2,1)S(1)}) custom-call(s32[5]{0:T(128)S(1)} %stack.23.core_ref.info_ref, bf16[8,520,128]{2,1,0:T(8,128)(2,1)S(1)} %all-to-all-done.stay_ref, bf16[8,256,128]{2,1,0:T(8,128)(2,1)S(1)} %collective-permute-done.2.cross_ref, ...), custom_call_target="tpu_custom_call" | custom-call | tf_op jit(solution)/shard_map/pallas_call | solution.py:300
  115.1 0.0 copy-start
  115.1 2.1 %collective-permute-start.14 = (f32[256,1536]{1,0:T(8,128)S(1)}, f32[256,1536]{1,0:T(8,128)S(1)}, u32[]{:S(2)}, u32[]{:S(2)}) collective-permute-start(f32[256,1536]{1,0:T(8,128)S(1)} %get-tuple-element.14), channel_id=1, source_target_pairs={{1,0},{0,1},{3,2},{2,3},{5,4},{4,5},{7,6},{6,7},{9,8},{8,9},{11,10... | collective-permute-start | bytes 4718600 | tf_op jit(solution)/shard_map/ppermute | solution.py:309
  117.1 1.1 shard_map.70
  118.3 25.2 %all_to_all.20 = bf16[8,264,128]{2,1,0:T(8,128)(2,1)S(1)} all-to-all(bf16[8,264,128]{2,1,0:T(8,128)(2,1)S(1)} %shard_map.70), channel_id=1, replica_groups=mesh['zh'=2,'y'=8,'zl'=4,'x'=4,'c'=2] {'y'}, dimensions={0} | all-to-all | bytes 1081344 | tf_op jit(solution)/shard_map/all_to_all | solution.py:286
  143.5 8.8 %collective-permute-start.1 = (bf16[8,264,128]{2,1,0:T(8,128)(2,1)S(1)}, bf16[8,264,128]{2,1,0:T(8,128)(2,1)S(1)}, u32[]{:S(2)}, u32[]{:S(2)}) collective-permute-start(bf16[8,264,128]{2,1,0:T(8,128)(2,1)S(1)} %all_to_all.20), channel_id=1, source_target_pairs={{256,0},{0,256},{257,1},{1,257},{258,2},{2,258},{259,3},{3,259},{2... | collective-permute-start | bytes 1622024 | tf_op jit(solution)/shard_map/ppermute | solution.py:289
  152.3 0.8 shard_map.74
  153.1 23.1 %collective-permute-done.1.cross_ref = bf16[8,264,128]{2,1,0:T(8,128)(2,1)S(1)} collective-permute-done((bf16[8,264,128]{2,1,0:T(8,128)(2,1)S(1)}, bf16[8,264,128]{2,1,0:T(8,128)(2,1)S(1)}, u32[]{:S(2)}, u32[]{:S(2)}) %collective-permute-start.1) | collective-permute-done | bytes 540704 | tf_op jit(solution)/shard_map/ppermute | solution.py:289
  176.2 3.2 %shard_map.73.mine_ref = f32[256,1536]{1,0:T(8,128)S(1)} custom-call(s32[5]{0:T(128)S(1)} %stack.23.core_ref.info_ref, bf16[8,520,128]{2,1,0:T(8,128)(2,1)S(1)} %all-to-all-done.stay_ref, bf16[8,264,128]{2,1,0:T(8,128)(2,1)S(1)} %collective-permute-done.1.cross_ref, bf16[1536,2048]{1,0:T(8,128)(2,1)S(1)} %get-tuple-element.13.whole_ref), custom_call_target="tpu_custom_call" | custom-call | tf_op jit(solution)/shard_map/pallas_call | solution.py:310
  179.5 0.0 collective-permute-done.14.theirs_ref
  179.5 0.0 copy-start.1
  179.5 2.6 %shard_map.75 = (bf16[256,3072]{1,0:T(8,128)(2,1)}, f32[16,8,128]{2,1,0:T(8,128)S(1)}) custom-call(s32[5]{0:T(128)S(1)} %stack.23.core_ref.info_ref, f32[256,1536]{1,0:T(8,128)S(1)} %shard_map.73.mine_ref, f32[256,1536]{1,0:T(8,128)S(1)} %collective-permute-done.14.theirs_ref, f32[256,1536]{1,0:T(8,128)S(1)} %get-tuple-element.15.gate_slope_ref, ...), custom_call_target="tpu_custom_call" | custom-call | tf_op jit(solution)/shard_map/pallas_call | solution.py:332
  182.0 18.8 %all_to_all.21.back_ref = f32[16,8,128]{2,1,0:T(8,128)S(1)} all-to-all(f32[16,8,128]{2,1,0:T(8,128)S(1)} %get-tuple-element.19), channel_id=1, replica_groups=mesh['zh'=2,'y'=8,'zl'=4,'x'=4,'c'=2] {'zh','y'}, dimensions={0} | all-to-all | bytes 131072 | tf_op jit(solution)/shard_map/all_to_all | solution.py:345
  200.9 0.8 shard_map.76
  (27 shorter events, 0.1 us)
Async XLA Ops:
  2.2 3.9 %collective-permute-start = (bf16[144,2048]{1,0:T(8,128)(2,1)S(1)}, bf16[144,2048]{1,0:T(8,128)(2,1)S(1)}, u32[]{:S(2)}, u32[]{:S(2)}) collective-permute-start(bf16[144,2048]{1,0:T(8,128)(2,1)S(1)} %get-tuple-element.11), channel_id=1, source_target_pairs={{1,0},{0,1},{3,2},{2,3},{5,4},{4,5},{7,6},{6,7},{9,8},{8,9},{11,10... | collective-permute-start | bytes 1769480 | tf_op jit(solution)/shard_map/ppermute | solution.py:274
  8.1 24.9 %all-to-all-start.2 = ((bf16[8,256,128]{2,1,0:T(8,128)(2,1)}), bf16[8,256,128]{2,1,0:T(8,128)(2,1)S(1)}, u32[]{:S(2)}, u32[]{:S(2)}) async-start(bf16[8,256,128]{2,1,0:T(8,128)(2,1)} %shard_map.71), calls=%async_computation.2 | async-start | bytes 1048576 | tf_op jit(solution)/shard_map/all_to_all | solution.py:286
  15.2 21.4 %collective-permute-start.3 = (bf16[1,1536,128]{2,1,0:T(8,128)(2,1)}, bf16[1,1536,128]{2,1,0:T(8,128)(2,1)}, u32[]{:S(2)}, u32[]{:S(2)}) collective-permute-start(bf16[1,1536,128]{2,1,0:T(8,128)(2,1)} %param.9), channel_id=1, source_target_pairs={{8,0},{16,8},{24,16},{0,24},{9,1},{17,9},{25,17},{1,25},{10,2},{18... | collective-permute-start | bytes 1179656 | tf_op jit(solution)/shard_map/ppermute | solution.py:238
  17.1 21.4 %collective-permute-start.4 = (bf16[1,1536,128]{2,1,0:T(8,128)(2,1)}, bf16[1,1536,128]{2,1,0:T(8,128)(2,1)S(1)}, u32[]{:S(2)}, u32[]{:S(2)}) collective-permute-start(bf16[1,1536,128]{2,1,0:T(8,128)(2,1)} %param.9), channel_id=1, source_target_pairs={{24,0},{0,8},{8,16},{16,24},{25,1},{1,9},{9,17},{17,25},{26,2},{2,... | collective-permute-start | bytes 1179656 | tf_op jit(solution)/shard_map/ppermute | solution.py:238
  32.9 77.0 %all-to-all-start = ((bf16[8,520,128]{2,1,0:T(8,128)(2,1)}), bf16[8,520,128]{2,1,0:T(8,128)(2,1)S(1)}, u32[]{:S(2)}, u32[]{:S(2)}) async-start(bf16[8,520,128]{2,1,0:T(8,128)(2,1)} %shard_map.69), calls=%async_computation | async-start | bytes 2129920 | tf_op jit(solution)/shard_map/all_to_all | solution.py:286
  39.3 39.8 %collective-permute-start.5 = (bf16[3,1536,128]{2,1,0:T(8,128)(2,1)}, bf16[3,1536,128]{2,1,0:T(8,128)(2,1)S(1)}, u32[]{:S(2)}, u32[]{:S(2)}) collective-permute-start(bf16[3,1536,128]{2,1,0:T(8,128)(2,1)} %constant_dynamic-update-slice_fusion.refs_0_), channel_id=1, source_target_pairs={{2,0},{4,2},{6,4},{0,6},{3,1},{5,3},{7,5},{1,7},{10,8},{12,10},{14... | collective-permute-start | bytes 3538952 | tf_op jit(solution)/shard_map/ppermute | solution.py:238
  43.9 39.3 %collective-permute-start.6 = (bf16[3,1536,128]{2,1,0:T(8,128)(2,1)}, bf16[3,1536,128]{2,1,0:T(8,128)(2,1)S(1)}, u32[]{:S(2)}, u32[]{:S(2)}) collective-permute-start(bf16[3,1536,128]{2,1,0:T(8,128)(2,1)} %constant_dynamic-update-slice_fusion.refs_0_), channel_id=1, source_target_pairs={{6,0},{0,2},{2,4},{4,6},{7,1},{1,3},{3,5},{5,7},{14,8},{8,10},{10,... | collective-permute-start | bytes 3538952 | tf_op jit(solution)/shard_map/ppermute | solution.py:238
  45.8 19.2 %collective-permute-start.7 = (bf16[1,1536,128]{2,1,0:T(8,128)(2,1)}, bf16[1,1536,128]{2,1,0:T(8,128)(2,1)S(1)}, u32[]{:S(2)}, u32[]{:S(2)}) collective-permute-start(bf16[1,1536,128]{2,1,0:T(8,128)(2,1)} %param.9), channel_id=1, source_target_pairs={{16,0},{24,8},{0,16},{8,24},{17,1},{25,9},{1,17},{9,25},{18,2},{26... | collective-permute-start | bytes 1179656 | tf_op jit(solution)/shard_map/ppermute | solution.py:238
  48.8 39.1 %collective-permute-start.11 = (bf16[1,1536,128]{2,1,0:T(8,128)(2,1)}, bf16[1,1536,128]{2,1,0:T(8,128)(2,1)S(1)}, u32[]{:S(2)}, u32[]{:S(2)}) collective-permute-start(bf16[1,1536,128]{2,1,0:T(8,128)(2,1)} %param.9), channel_id=1, source_target_pairs={{4,0},{6,2},{0,4},{2,6},{5,1},{7,3},{1,5},{3,7},{12,8},{14,10},{8,... | collective-permute-start | bytes 1179656 | tf_op jit(solution)/shard_map/ppermute | solution.py:238
  65.1 44.1 %copy-start.4 = (bf16[1,1536,128]{2,1,0:T(8,128)(2,1)}, bf16[1,1536,128]{2,1,0:T(8,128)(2,1)S(1)}, u32[]{:S(2)}) copy-start(bf16[1,1536,128]{2,1,0:T(8,128)(2,1)S(1)} %collective-permute-done.7.refs_3_) | copy-start | bytes 1179652
  65.1 29.6 %collective-permute-start.8 = (bf16[1,1536,128]{2,1,0:T(8,128)(2,1)S(1)}, bf16[1,1536,128]{2,1,0:T(8,128)(2,1)S(1)}, u32[]{:S(2)}, u32[]{:S(2)}) collective-permute-start(bf16[1,1536,128]{2,1,0:T(8,128)(2,1)S(1)} %collective-permute-done.7.refs_3_), channel_id=1, source_target_pairs={{2,0},{4,2},{6,4},{0,6},{3,1},{5,3},{7,5},{1,7},{10,8},{12,10},{14... | collective-permute-start | bytes 1179656 | tf_op jit(solution)/shard_map/ppermute | solution.py:238
  69.9 40.0 %collective-permute-start.2 = (bf16[8,256,128]{2,1,0:T(8,128)(2,1)S(1)}, bf16[8,256,128]{2,1,0:T(8,128)(2,1)S(1)}, u32[]{:S(2)}, u32[]{:S(2)}) collective-permute-start(bf16[8,256,128]{2,1,0:T(8,128)(2,1)S(1)} %all-to-all-done.2), channel_id=1, source_target_pairs={{256,0},{0,256},{257,1},{1,257},{258,2},{2,258},{259,3},{3,259},{2... | collective-permute-start | bytes 1572872 | tf_op jit(solution)/shard_map/ppermute | solution.py:289
  79.1 30.1 %copy-start.2 = (bf16[3,1536,128]{2,1,0:T(8,128)(2,1)}, bf16[3,1536,128]{2,1,0:T(8,128)(2,1)S(1)}, u32[]{:S(2)}) copy-start(bf16[3,1536,128]{2,1,0:T(8,128)(2,1)S(1)} %collective-permute-done.5.refs_1_) | copy-start | bytes 3538948
  79.1 17.5 %collective-permute-start.9 = (bf16[1,1536,128]{2,1,0:T(8,128)(2,1)S(1)}, bf16[1,1536,128]{2,1,0:T(8,128)(2,1)S(1)}, u32[]{:S(2)}, u32[]{:S(2)}) collective-permute-start(bf16[1,1536,128]{2,1,0:T(8,128)(2,1)S(1)} %collective-permute-done.7.refs_3_), channel_id=1, source_target_pairs={{6,0},{0,2},{2,4},{4,6},{7,1},{1,3},{3,5},{5,7},{14,8},{8,10},{10,... | collective-permute-start | bytes 1179656 | tf_op jit(solution)/shard_map/ppermute | solution.py:238
  83.2 26.0 %copy-start.3 = (bf16[3,1536,128]{2,1,0:T(8,128)(2,1)}, bf16[3,1536,128]{2,1,0:T(8,128)(2,1)S(1)}, u32[]{:S(2)}) copy-start(bf16[3,1536,128]{2,1,0:T(8,128)(2,1)S(1)} %collective-permute-done.6.refs_2_) | copy-start | bytes 3538948
  83.2 19.3 %collective-permute-start.10 = (bf16[1,1536,128]{2,1,0:T(8,128)(2,1)S(1)}, bf16[1,1536,128]{2,1,0:T(8,128)(2,1)S(1)}, u32[]{:S(2)}, u32[]{:S(2)}) collective-permute-start(bf16[1,1536,128]{2,1,0:T(8,128)(2,1)S(1)} %collective-permute-done.7.refs_3_), channel_id=1, source_target_pairs={{4,0},{6,2},{0,4},{2,6},{5,1},{7,3},{1,5},{3,7},{12,8},{14,10},{8,... | collective-permute-start | bytes 1179656 | tf_op jit(solution)/shard_map/ppermute | solution.py:238
  88.0 21.2 %copy-start.5 = (bf16[1,1536,128]{2,1,0:T(8,128)(2,1)}, bf16[1,1536,128]{2,1,0:T(8,128)(2,1)S(1)}, u32[]{:S(2)}) copy-start(bf16[1,1536,128]{2,1,0:T(8,128)(2,1)S(1)} %collective-permute-done.11.refs_7_) | copy-start | bytes 1179652
  88.0 15.2 %collective-permute-start.12 = (bf16[1,1536,128]{2,1,0:T(8,128)(2,1)S(1)}, bf16[1,1536,128]{2,1,0:T(8,128)(2,1)S(1)}, u32[]{:S(2)}, u32[]{:S(2)}) collective-permute-start(bf16[1,1536,128]{2,1,0:T(8,128)(2,1)S(1)} %slice.16), channel_id=1, source_target_pairs={{2,0},{4,2},{6,4},{0,6},{3,1},{5,3},{7,5},{1,7},{10,8},{12,10},{14... | collective-permute-start | bytes 1179656 | tf_op jit(solution)/shard_map/ppermute | solution.py:238
  94.7 14.5 %copy-start.6 = (bf16[1,1536,128]{2,1,0:T(8,128)(2,1)}, bf16[1,1536,128]{2,1,0:T(8,128)(2,1)S(1)}, u32[]{:S(2)}) copy-start(bf16[1,1536,128]{2,1,0:T(8,128)(2,1)S(1)} %collective-permute-done.8.refs_4_) | copy-start | bytes 1179652
  94.7 14.4 %collective-permute-start.13 = (bf16[1,1536,128]{2,1,0:T(8,128)(2,1)S(1)}, bf16[1,1536,128]{2,1,0:T(8,128)(2,1)S(1)}, u32[]{:S(2)}, u32[]{:S(2)}) collective-permute-start(bf16[1,1536,128]{2,1,0:T(8,128)(2,1)S(1)} %slice.17), channel_id=1, source_target_pairs={{6,0},{0,2},{2,4},{4,6},{7,1},{1,3},{3,5},{5,7},{14,8},{8,10},{10,... | collective-permute-start | bytes 1179656 | tf_op jit(solution)/shard_map/ppermute | solution.py:238
  96.7 12.5 %copy-start.7 = (bf16[1,1536,128]{2,1,0:T(8,128)(2,1)}, bf16[1,1536,128]{2,1,0:T(8,128)(2,1)S(1)}, u32[]{:S(2)}) copy-start(bf16[1,1536,128]{2,1,0:T(8,128)(2,1)S(1)} %collective-permute-done.9.refs_5_) | copy-start | bytes 1179652
  102.5 6.7 %copy-start.8 = (bf16[1,1536,128]{2,1,0:T(8,128)(2,1)}, bf16[1,1536,128]{2,1,0:T(8,128)(2,1)S(1)}, u32[]{:S(2)}) copy-start(bf16[1,1536,128]{2,1,0:T(8,128)(2,1)S(1)} %collective-permute-done.10.refs_6_) | copy-start | bytes 1179652
  103.2 6.0 %copy-start.9 = (bf16[1,1536,128]{2,1,0:T(8,128)(2,1)}, bf16[1,1536,128]{2,1,0:T(8,128)(2,1)S(1)}, u32[]{:S(2)}) copy-start(bf16[1,1536,128]{2,1,0:T(8,128)(2,1)S(1)} %collective-permute-done.12.refs_8_) | copy-start | bytes 1179652
  109.2 0.7 copy-start.10
  115.1 37.2 %copy-start = (bf16[1,1,256,3072]{3,2,1,0:T(8,128)(2,1)S(1)}, bf16[1,1,256,3072]{3,2,1,0:T(8,128)(2,1)}, u32[]{:S(2)}) copy-start(bf16[1,1,256,3072]{3,2,1,0:T(8,128)(2,1)} %param.8) | copy-start | bytes 4718596
  115.1 64.4 %collective-permute-start.14 = (f32[256,1536]{1,0:T(8,128)S(1)}, f32[256,1536]{1,0:T(8,128)S(1)}, u32[]{:S(2)}, u32[]{:S(2)}) collective-permute-start(f32[256,1536]{1,0:T(8,128)S(1)} %get-tuple-element.14), channel_id=1, source_target_pairs={{1,0},{0,1},{3,2},{2,3},{5,4},{4,5},{7,6},{6,7},{9,8},{8,9},{11,10... | collective-permute-start | bytes 4718600 | tf_op jit(solution)/shard_map/ppermute | solution.py:309
  143.5 32.7 %collective-permute-start.1 = (bf16[8,264,128]{2,1,0:T(8,128)(2,1)S(1)}, bf16[8,264,128]{2,1,0:T(8,128)(2,1)S(1)}, u32[]{:S(2)}, u32[]{:S(2)}) collective-permute-start(bf16[8,264,128]{2,1,0:T(8,128)(2,1)S(1)} %all_to_all.20), channel_id=1, source_target_pairs={{256,0},{0,256},{257,1},{1,257},{258,2},{2,258},{259,3},{3,259},{2... | collective-permute-start | bytes 1622024 | tf_op jit(solution)/shard_map/ppermute | solution.py:289
  179.5 21.4 %copy-start.1 = (s32[128,8]{0,1:T(8,128)S(1)}, s32[128,8]{0,1:T(8,128)}, u32[]{:S(2)}) copy-start(s32[128,8]{0,1:T(8,128)} %param.6) | copy-start | bytes 12292

commit v4 on v2

--- a/solution.py
+++ b/solution.py
@@ -163,7 +163,7 @@
     here = pl.ds(pl.multiple_of(number * rows, rows), rows)
     sources = score_ref.shape[0]
     step = 256
-    total = jnp.zeros((rows, 1), F32)
+    total = jnp.zeros((rows, LANES), F32)
     line = jnp.where(number < 2, stay_ref[...].astype(F32), cross_ref[...].astype(F32))
     gate_in = to_column(line[:, :1, :], rows // sources)
     for j in range(units // step):
@@ -175,10 +175,12 @@
         sig = 1.0 / (1.0 + jnp.exp(-a))
         silu = a * sig
         hidden = (silu * u).astype(BF16).astype(F32)
-        total += jnp.sum(grad * hidden, axis=1, keepdims=True)
+        terms = grad * hidden
+        total += terms[:, :LANES] + terms[:, LANES:]
         scaled = grad * gate_in
         out_ref[:, cols] = (scaled * u * sig * (1.0 + a * (1.0 - sig))).astype(BF16)
         out_ref[:, up_cols] = (scaled * silu).astype(BF16)
+    total = jnp.sum(total, axis=1, keepdims=True)
     score_ref[...] = jnp.broadcast_to(to_lanes(total, sources), score_ref.shape)
 
 

time: 203 us -> 203 us (level)
  no operation moved by 1% of the time
where the time goes in v4:
time: 203 us; the launch traced here: 202 us
  starting transfers between devices  67.6 us (33%)
  waiting for transfers between devices  65.1 us (32%)
  blocking collectives  44.1 us (22%)
  Pallas kernels  19.1 us (9%)
  local copies, waits for them, and re-layouts  5.26 us (3%)
    ppermute x11, starting transfers between devices, permute(): return lax.ppermute(array, axis, ring(4, shift))  35.2 us
    ppermute x11, waiting for transfers between devices, permute(): return lax.ppermute(array, axis, ring(4, shift))  31.7 us
    all_to_all x1, blocking collectives, along_y(): return lax.all_to_all(array, 'y', split_axis=0, concat_axis=0, tiled=True)  25.2 us
    ppermute x2, waiting for transfers between devices, across(): return lax.ppermute(array, 'zh', ring(2, 1))  24 us
    all_to_all x1, blocking collectives, step(): back = lax.all_to_all(score, EP, split_axis=0, concat_axis=0, tiled=True)  18.9 us
    ppermute x2, starting transfers between devices, across(): return lax.ppermute(array, 'zh', ring(2, 1))  17.9 us
    all_to_all x2, starting transfers between devices, along_y(): return lax.all_to_all(array, 'y', split_axis=0, concat_axis=0, tiled=True)  10.7 us
    all_to_all x2, waiting for transfers between devices, along_y(): return lax.all_to_all(array, 'y', split_axis=0, concat_axis=0, tiled=True)  7.45 us
  transfers between devices with their start and end apart: 17, of which 10 were waited for; matrix products, arithmetic and copies ran while one was open for 2% of the time, Pallas kernels for 3%

profile of v4, /device:TPU:128, one launch (start us, length us, event | category | flops | bytes accessed | tf_op | source)
XLA Modules:
  0.0 202.1 jit_solution(18008037133308982342)
XLA Ops:
  0.6 0.1 stack.23.core_ref.info_ref
  0.7 1.5 shard_map.68
  2.2 1.9 collective-permute-start
  4.2 2.0 collective-permute-done.got_ref
  6.1 1.9 shard_map.71
  8.1 7.1 %all-to-all-start.2 = ((bf16[8,256,128]{2,1,0:T(8,128)(2,1)}), bf16[8,256,128]{2,1,0:T(8,128)(2,1)S(1)}, u32[]{:S(2)}, u32[]{:S(2)}) async-start(bf16[8,256,128]{2,1,0:T(8,128)(2,1)} %shard_map.71), calls=%async_computation.2 | async-start | bytes 1048576 | tf_op jit(solution)/shard_map/all_to_all | solution.py:270
  15.2 1.9 collective-permute-start.3
  17.1 4.3 %collective-permute-start.4 = (bf16[1,1536,128]{2,1,0:T(8,128)(2,1)}, bf16[1,1536,128]{2,1,0:T(8,128)(2,1)S(1)}, u32[]{:S(2)}, u32[]{:S(2)}) collective-permute-start(bf16[1,1536,128]{2,1,0:T(8,128)(2,1)} %param.9), channel_id=1, source_target_pairs={{24,0},{0,8},{8,16},{16,24},{25,1},{1,9},{9,17},{17,25},{26,2},{2,... | collective-permute-start | bytes 1179656 | tf_op jit(solution)/shard_map/ppermute | solution.py:222
  21.4 1.8 constant_dynamic-update-slice_fusion.2
  23.2 2.4 %shard_map.69 = bf16[8,520,128]{2,1,0:T(8,128)(2,1)} custom-call(s32[5]{0:T(128)S(1)} %stack.23.core_ref.info_ref, bf16[144,2048]{1,0:T(8,128)(2,1)S(1)} %collective-permute-done.got_ref, bf16[128,2048]{1,0:T(8,128)(2,1)S(1)} %get-tuple-element.9.keep_ref, s32[8,128]{1,0:T(8,128)} %bitcast.13, bf16[8,128]{1,0:T(8,128)(2,1)} %bitcast.17), custom_call_target="tpu_custom_call" | custom-call | tf_op jit(solution)/shard_map/pallas_call | solution.py:264
  25.5 7.5 %all-to-all-done.2 = bf16[8,256,128]{2,1,0:T(8,128)(2,1)S(1)} async-done(((bf16[8,256,128]{2,1,0:T(8,128)(2,1)}), bf16[8,256,128]{2,1,0:T(8,128)(2,1)S(1)}, u32[]{:S(2)}, u32[]{:S(2)}) %all-to-all-start.2) | async-done | bytes 524320 | tf_op jit(solution)/shard_map/all_to_all | solution.py:270
  33.0 3.6 %all-to-all-start = ((bf16[8,520,128]{2,1,0:T(8,128)(2,1)}), bf16[8,520,128]{2,1,0:T(8,128)(2,1)S(1)}, u32[]{:S(2)}, u32[]{:S(2)}) async-start(bf16[8,520,128]{2,1,0:T(8,128)(2,1)} %shard_map.69), calls=%async_computation | async-start | bytes 2129920 | tf_op jit(solution)/shard_map/all_to_all | solution.py:270
  36.5 0.0 collective-permute-done.3
  36.5 1.8 constant_dynamic-update-slice_fusion.1
  38.3 0.2 collective-permute-done.4
  38.5 0.8 constant_dynamic-update-slice_fusion.refs_0_
  39.3 4.7 %collective-permute-start.5 = (bf16[3,1536,128]{2,1,0:T(8,128)(2,1)}, bf16[3,1536,128]{2,1,0:T(8,128)(2,1)S(1)}, u32[]{:S(2)}, u32[]{:S(2)}) collective-permute-start(bf16[3,1536,128]{2,1,0:T(8,128)(2,1)} %constant_dynamic-update-slice_fusion.refs_0_), channel_id=1, source_target_pairs={{2,0},{4,2},{6,4},{0,6},{3,1},{5,3},{7,5},{1,7},{10,8},{12,10},{14... | collective-permute-start | bytes 3538952 | tf_op jit(solution)/shard_map/ppermute | solution.py:222
  43.9 1.9 collective-permute-start.6
  45.9 3.0 %collective-permute-start.7 = (bf16[1,1536,128]{2,1,0:T(8,128)(2,1)}, bf16[1,1536,128]{2,1,0:T(8,128)(2,1)S(1)}, u32[]{:S(2)}, u32[]{:S(2)}) collective-permute-start(bf16[1,1536,128]{2,1,0:T(8,128)(2,1)} %param.9), channel_id=1, source_target_pairs={{16,0},{24,8},{0,16},{8,24},{17,1},{25,9},{1,17},{9,25},{18,2},{26... | collective-permute-start | bytes 1179656 | tf_op jit(solution)/shard_map/ppermute | solution.py:222
  48.9 4.2 %collective-permute-start.11 = (bf16[1,1536,128]{2,1,0:T(8,128)(2,1)}, bf16[1,1536,128]{2,1,0:T(8,128)(2,1)S(1)}, u32[]{:S(2)}, u32[]{:S(2)}) collective-permute-start(bf16[1,1536,128]{2,1,0:T(8,128)(2,1)} %param.9), channel_id=1, source_target_pairs={{4,0},{6,2},{0,4},{2,6},{5,1},{7,3},{1,5},{3,7},{12,8},{14,10},{8,... | collective-permute-start | bytes 1179656 | tf_op jit(solution)/shard_map/ppermute | solution.py:222
  53.0 12.1 %collective-permute-done.7.refs_3_ = bf16[1,1536,128]{2,1,0:T(8,128)(2,1)S(1)} collective-permute-done((bf16[1,1536,128]{2,1,0:T(8,128)(2,1)}, bf16[1,1536,128]{2,1,0:T(8,128)(2,1)S(1)}, u32[]{:S(2)}, u32[]{:S(2)}) %collective-permute-start.7) | collective-permute-done | bytes 393248 | tf_op jit(solution)/shard_map/ppermute | solution.py:222
  65.1 4.8 %collective-permute-start.8 = (bf16[1,1536,128]{2,1,0:T(8,128)(2,1)S(1)}, bf16[1,1536,128]{2,1,0:T(8,128)(2,1)S(1)}, u32[]{:S(2)}, u32[]{:S(2)}) collective-permute-start(bf16[1,1536,128]{2,1,0:T(8,128)(2,1)S(1)} %collective-permute-done.7.refs_3_), channel_id=1, source_target_pairs={{2,0},{4,2},{6,4},{0,6},{3,1},{5,3},{7,5},{1,7},{10,8},{12,10},{14... | collective-permute-start | bytes 1179656 | tf_op jit(solution)/shard_map/ppermute | solution.py:222
  70.0 9.1 %collective-permute-start.2 = (bf16[8,256,128]{2,1,0:T(8,128)(2,1)S(1)}, bf16[8,256,128]{2,1,0:T(8,128)(2,1)S(1)}, u32[]{:S(2)}, u32[]{:S(2)}) collective-permute-start(bf16[8,256,128]{2,1,0:T(8,128)(2,1)S(1)} %all-to-all-done.2), channel_id=1, source_target_pairs={{256,0},{0,256},{257,1},{1,257},{258,2},{2,258},{259,3},{3,259},{2... | collective-permute-start | bytes 1572872 | tf_op jit(solution)/shard_map/ppermute | solution.py:273
  79.1 1.9 collective-permute-start.9
  81.1 2.2 %collective-permute-done.6.refs_2_ = bf16[3,1536,128]{2,1,0:T(8,128)(2,1)S(1)} collective-permute-done((bf16[3,1536,128]{2,1,0:T(8,128)(2,1)}, bf16[3,1536,128]{2,1,0:T(8,128)(2,1)S(1)}, u32[]{:S(2)}, u32[]{:S(2)}) %collective-permute-start.6) | collective-permute-done | bytes 1179680 | tf_op jit(solution)/shard_map/ppermute | solution.py:222
  83.3 4.7 %collective-permute-start.10 = (bf16[1,1536,128]{2,1,0:T(8,128)(2,1)S(1)}, bf16[1,1536,128]{2,1,0:T(8,128)(2,1)S(1)}, u32[]{:S(2)}, u32[]{:S(2)}) collective-permute-start(bf16[1,1536,128]{2,1,0:T(8,128)(2,1)S(1)} %collective-permute-done.7.refs_3_), channel_id=1, source_target_pairs={{4,0},{6,2},{0,4},{2,6},{5,1},{7,3},{1,5},{3,7},{12,8},{14,10},{8,... | collective-permute-start | bytes 1179656 | tf_op jit(solution)/shard_map/ppermute | solution.py:222
  88.0 0.0 collective-permute-done.11.refs_7_
  88.0 1.9 collective-permute-start.12
  89.9 4.8 %collective-permute-done.8.refs_4_ = bf16[1,1536,128]{2,1,0:T(8,128)(2,1)S(1)} collective-permute-done((bf16[1,1536,128]{2,1,0:T(8,128)(2,1)S(1)}, bf16[1,1536,128]{2,1,0:T(8,128)(2,1)S(1)}, u32[]{:S(2)}, u32[]{:S(2)}) %collective-permute-start.8) | collective-permute-done | bytes 393248 | tf_op jit(solution)/shard_map/ppermute | solution.py:222
  94.8 1.9 collective-permute-start.13
  96.7 0.0 collective-permute-done.9.refs_5_
  96.7 5.8 %collective-permute-done.10.refs_6_ = bf16[1,1536,128]{2,1,0:T(8,128)(2,1)S(1)} collective-permute-done((bf16[1,1536,128]{2,1,0:T(8,128)(2,1)S(1)}, bf16[1,1536,128]{2,1,0:T(8,128)(2,1)S(1)}, u32[]{:S(2)}, u32[]{:S(2)}) %collective-permute-start.10) | collective-permute-done | bytes 393248 | tf_op jit(solution)/shard_map/ppermute | solution.py:222
  102.5 0.7 collective-permute-done.12.refs_8_
  103.2 6.0 %collective-permute-done.13.refs_9_ = bf16[1,1536,128]{2,1,0:T(8,128)(2,1)S(1)} collective-permute-done((bf16[1,1536,128]{2,1,0:T(8,128)(2,1)S(1)}, bf16[1,1536,128]{2,1,0:T(8,128)(2,1)S(1)}, u32[]{:S(2)}, u32[]{:S(2)}) %collective-permute-start.13) | collective-permute-done | bytes 393248 | tf_op jit(solution)/shard_map/ppermute | solution.py:222
  109.3 0.8 copy-done.10
  110.0 0.0 collective-permute-done.2.cross_ref
  110.0 5.1 %shard_map.72 = (f32[256,1536]{1,0:T(8,128)S(1)}, bf16[1536,2048]{1,0:T(8,128)(2,1)S(1)}) custom-call(s32[5]{0:T(128)S(1)} %stack.23.core_ref.info_ref, bf16[8,520,128]{2,1,0:T(8,128)(2,1)S(1)} %all-to-all-done.stay_ref, bf16[8,256,128]{2,1,0:T(8,128)(2,1)S(1)} %collective-permute-done.2.cross_ref, ...), custom_call_target="tpu_custom_call" | custom-call | tf_op jit(solution)/shard_map/pallas_call | solution.py:284
  115.1 1.9 collective-permute-start.14
  117.0 1.1 shard_map.70
  118.2 25.2 %all_to_all.20 = bf16[8,264,128]{2,1,0:T(8,128)(2,1)S(1)} all-to-all(bf16[8,264,128]{2,1,0:T(8,128)(2,1)S(1)} %shard_map.70), channel_id=1, replica_groups=mesh['zh'=2,'y'=8,'zl'=4,'x'=4,'c'=2] {'y'}, dimensions={0} | all-to-all | bytes 1081344 | tf_op jit(solution)/shard_map/all_to_all | solution.py:270
  143.4 8.8 %collective-permute-start.1 = (bf16[8,264,128]{2,1,0:T(8,128)(2,1)S(1)}, bf16[8,264,128]{2,1,0:T(8,128)(2,1)S(1)}, u32[]{:S(2)}, u32[]{:S(2)}) collective-permute-start(bf16[8,264,128]{2,1,0:T(8,128)(2,1)S(1)} %all_to_all.20), channel_id=1, source_target_pairs={{256,0},{0,256},{257,1},{1,257},{258,2},{2,258},{259,3},{3,259},{2... | collective-permute-start | bytes 1622024 | tf_op jit(solution)/shard_map/ppermute | solution.py:273
  152.1 24.0 %collective-permute-done.1.cross_ref = bf16[8,264,128]{2,1,0:T(8,128)(2,1)S(1)} collective-permute-done((bf16[8,264,128]{2,1,0:T(8,128)(2,1)S(1)}, bf16[8,264,128]{2,1,0:T(8,128)(2,1)S(1)}, u32[]{:S(2)}, u32[]{:S(2)}) %collective-permute-start.1) | collective-permute-done | bytes 540704 | tf_op jit(solution)/shard_map/ppermute | solution.py:273
  176.1 3.3 %shard_map.73.mine_ref = f32[256,1536]{1,0:T(8,128)S(1)} custom-call(s32[5]{0:T(128)S(1)} %stack.23.core_ref.info_ref, bf16[8,520,128]{2,1,0:T(8,128)(2,1)S(1)} %all-to-all-done.stay_ref, bf16[8,264,128]{2,1,0:T(8,128)(2,1)S(1)} %collective-permute-done.1.cross_ref, bf16[1536,2048]{1,0:T(8,128)(2,1)S(1)} %get-tuple-element.10.whole_ref), custom_call_target="tpu_custom_call" | custom-call | tf_op jit(solution)/shard_map/pallas_call | solution.py:294
  179.4 0.0 collective-permute-done.14.theirs_ref
  179.4 0.0 copy-start.1
  179.4 3.0 %shard_map.74 = (bf16[256,3072]{1,0:T(8,128)(2,1)}, f32[16,8,128]{2,1,0:T(8,128)S(1)}) custom-call(s32[5]{0:T(128)S(1)} %stack.23.core_ref.info_ref, f32[256,1536]{1,0:T(8,128)S(1)} %shard_map.73.mine_ref, f32[256,1536]{1,0:T(8,128)S(1)} %collective-permute-done.14.theirs_ref, bf16[256,3072]{1,0:T(8,128)(2,1)S(1)} %bitcast.10, ...), custom_call_target="tpu_custom_call" | custom-call | tf_op jit(solution)/shard_map/pallas_call | solution.py:307
  182.5 18.9 %all_to_all.21.back_ref = f32[16,8,128]{2,1,0:T(8,128)S(1)} all-to-all(f32[16,8,128]{2,1,0:T(8,128)S(1)} %get-tuple-element.13), channel_id=1, replica_groups=mesh['zh'=2,'y'=8,'zl'=4,'x'=4,'c'=2] {'zh','y'}, dimensions={0} | all-to-all | bytes 131072 | tf_op jit(solution)/shard_map/all_to_all | solution.py:318
  201.3 0.8 shard_map.75
  (26 shorter events, 0.1 us)
Async XLA Ops:
  2.2 3.9 %collective-permute-start = (bf16[144,2048]{1,0:T(8,128)(2,1)S(1)}, bf16[144,2048]{1,0:T(8,128)(2,1)S(1)}, u32[]{:S(2)}, u32[]{:S(2)}) collective-permute-start(bf16[144,2048]{1,0:T(8,128)(2,1)S(1)} %get-tuple-element.8), channel_id=1, source_target_pairs={{1,0},{0,1},{3,2},{2,3},{5,4},{4,5},{7,6},{6,7},{9,8},{8,9},{11,10... | collective-permute-start | bytes 1769480 | tf_op jit(solution)/shard_map/ppermute | solution.py:258
  8.1 24.9 %all-to-all-start.2 = ((bf16[8,256,128]{2,1,0:T(8,128)(2,1)}), bf16[8,256,128]{2,1,0:T(8,128)(2,1)S(1)}, u32[]{:S(2)}, u32[]{:S(2)}) async-start(bf16[8,256,128]{2,1,0:T(8,128)(2,1)} %shard_map.71), calls=%async_computation.2 | async-start | bytes 1048576 | tf_op jit(solution)/shard_map/all_to_all | solution.py:270
  15.2 21.4 %collective-permute-start.3 = (bf16[1,1536,128]{2,1,0:T(8,128)(2,1)}, bf16[1,1536,128]{2,1,0:T(8,128)(2,1)}, u32[]{:S(2)}, u32[]{:S(2)}) collective-permute-start(bf16[1,1536,128]{2,1,0:T(8,128)(2,1)} %param.9), channel_id=1, source_target_pairs={{8,0},{16,8},{24,16},{0,24},{9,1},{17,9},{25,17},{1,25},{10,2},{18... | collective-permute-start | bytes 1179656 | tf_op jit(solution)/shard_map/ppermute | solution.py:222
  17.1 21.4 %collective-permute-start.4 = (bf16[1,1536,128]{2,1,0:T(8,128)(2,1)}, bf16[1,1536,128]{2,1,0:T(8,128)(2,1)S(1)}, u32[]{:S(2)}, u32[]{:S(2)}) collective-permute-start(bf16[1,1536,128]{2,1,0:T(8,128)(2,1)} %param.9), channel_id=1, source_target_pairs={{24,0},{0,8},{8,16},{16,24},{25,1},{1,9},{9,17},{17,25},{26,2},{2,... | collective-permute-start | bytes 1179656 | tf_op jit(solution)/shard_map/ppermute | solution.py:222
  33.0 77.1 %all-to-all-start = ((bf16[8,520,128]{2,1,0:T(8,128)(2,1)}), bf16[8,520,128]{2,1,0:T(8,128)(2,1)S(1)}, u32[]{:S(2)}, u32[]{:S(2)}) async-start(bf16[8,520,128]{2,1,0:T(8,128)(2,1)} %shard_map.69), calls=%async_computation | async-start | bytes 2129920 | tf_op jit(solution)/shard_map/all_to_all | solution.py:270
  39.3 39.8 %collective-permute-start.5 = (bf16[3,1536,128]{2,1,0:T(8,128)(2,1)}, bf16[3,1536,128]{2,1,0:T(8,128)(2,1)S(1)}, u32[]{:S(2)}, u32[]{:S(2)}) collective-permute-start(bf16[3,1536,128]{2,1,0:T(8,128)(2,1)} %constant_dynamic-update-slice_fusion.refs_0_), channel_id=1, source_target_pairs={{2,0},{4,2},{6,4},{0,6},{3,1},{5,3},{7,5},{1,7},{10,8},{12,10},{14... | collective-permute-start | bytes 3538952 | tf_op jit(solution)/shard_map/ppermute | solution.py:222
  43.9 39.3 %collective-permute-start.6 = (bf16[3,1536,128]{2,1,0:T(8,128)(2,1)}, bf16[3,1536,128]{2,1,0:T(8,128)(2,1)S(1)}, u32[]{:S(2)}, u32[]{:S(2)}) collective-permute-start(bf16[3,1536,128]{2,1,0:T(8,128)(2,1)} %constant_dynamic-update-slice_fusion.refs_0_), channel_id=1, source_target_pairs={{6,0},{0,2},{2,4},{4,6},{7,1},{1,3},{3,5},{5,7},{14,8},{8,10},{10,... | collective-permute-start | bytes 3538952 | tf_op jit(solution)/shard_map/ppermute | solution.py:222
  45.9 19.2 %collective-permute-start.7 = (bf16[1,1536,128]{2,1,0:T(8,128)(2,1)}, bf16[1,1536,128]{2,1,0:T(8,128)(2,1)S(1)}, u32[]{:S(2)}, u32[]{:S(2)}) collective-permute-start(bf16[1,1536,128]{2,1,0:T(8,128)(2,1)} %param.9), channel_id=1, source_target_pairs={{16,0},{24,8},{0,16},{8,24},{17,1},{25,9},{1,17},{9,25},{18,2},{26... | collective-permute-start | bytes 1179656 | tf_op jit(solution)/shard_map/ppermute | solution.py:222
  48.9 39.1 %collective-permute-start.11 = (bf16[1,1536,128]{2,1,0:T(8,128)(2,1)}, bf16[1,1536,128]{2,1,0:T(8,128)(2,1)S(1)}, u32[]{:S(2)}, u32[]{:S(2)}) collective-permute-start(bf16[1,1536,128]{2,1,0:T(8,128)(2,1)} %param.9), channel_id=1, source_target_pairs={{4,0},{6,2},{0,4},{2,6},{5,1},{7,3},{1,5},{3,7},{12,8},{14,10},{8,... | collective-permute-start | bytes 1179656 | tf_op jit(solution)/shard_map/ppermute | solution.py:222
  65.1 44.1 %copy-start.4 = (bf16[1,1536,128]{2,1,0:T(8,128)(2,1)}, bf16[1,1536,128]{2,1,0:T(8,128)(2,1)S(1)}, u32[]{:S(2)}) copy-start(bf16[1,1536,128]{2,1,0:T(8,128)(2,1)S(1)} %collective-permute-done.7.refs_3_) | copy-start | bytes 1179652
  65.1 29.6 %collective-permute-start.8 = (bf16[1,1536,128]{2,1,0:T(8,128)(2,1)S(1)}, bf16[1,1536,128]{2,1,0:T(8,128)(2,1)S(1)}, u32[]{:S(2)}, u32[]{:S(2)}) collective-permute-start(bf16[1,1536,128]{2,1,0:T(8,128)(2,1)S(1)} %collective-permute-done.7.refs_3_), channel_id=1, source_target_pairs={{2,0},{4,2},{6,4},{0,6},{3,1},{5,3},{7,5},{1,7},{10,8},{12,10},{14... | collective-permute-start | bytes 1179656 | tf_op jit(solution)/shard_map/ppermute | solution.py:222
  70.0 40.1 %collective-permute-start.2 = (bf16[8,256,128]{2,1,0:T(8,128)(2,1)S(1)}, bf16[8,256,128]{2,1,0:T(8,128)(2,1)S(1)}, u32[]{:S(2)}, u32[]{:S(2)}) collective-permute-start(bf16[8,256,128]{2,1,0:T(8,128)(2,1)S(1)} %all-to-all-done.2), channel_id=1, source_target_pairs={{256,0},{0,256},{257,1},{1,257},{258,2},{2,258},{259,3},{3,259},{2... | collective-permute-start | bytes 1572872 | tf_op jit(solution)/shard_map/ppermute | solution.py:273
  79.1 30.1 %copy-start.2 = (bf16[3,1536,128]{2,1,0:T(8,128)(2,1)}, bf16[3,1536,128]{2,1,0:T(8,128)(2,1)S(1)}, u32[]{:S(2)}) copy-start(bf16[3,1536,128]{2,1,0:T(8,128)(2,1)S(1)} %collective-permute-done.5.refs_1_) | copy-start | bytes 3538948
  79.1 17.5 %collective-permute-start.9 = (bf16[1,1536,128]{2,1,0:T(8,128)(2,1)S(1)}, bf16[1,1536,128]{2,1,0:T(8,128)(2,1)S(1)}, u32[]{:S(2)}, u32[]{:S(2)}) collective-permute-start(bf16[1,1536,128]{2,1,0:T(8,128)(2,1)S(1)} %collective-permute-done.7.refs_3_), channel_id=1, source_target_pairs={{6,0},{0,2},{2,4},{4,6},{7,1},{1,3},{3,5},{5,7},{14,8},{8,10},{10,... | collective-permute-start | bytes 1179656 | tf_op jit(solution)/shard_map/ppermute | solution.py:222
  83.3 26.0 %copy-start.3 = (bf16[3,1536,128]{2,1,0:T(8,128)(2,1)}, bf16[3,1536,128]{2,1,0:T(8,128)(2,1)S(1)}, u32[]{:S(2)}) copy-start(bf16[3,1536,128]{2,1,0:T(8,128)(2,1)S(1)} %collective-permute-done.6.refs_2_) | copy-start | bytes 3538948
  83.3 19.3 %collective-permute-start.10 = (bf16[1,1536,128]{2,1,0:T(8,128)(2,1)S(1)}, bf16[1,1536,128]{2,1,0:T(8,128)(2,1)S(1)}, u32[]{:S(2)}, u32[]{:S(2)}) collective-permute-start(bf16[1,1536,128]{2,1,0:T(8,128)(2,1)S(1)} %collective-permute-done.7.refs_3_), channel_id=1, source_target_pairs={{4,0},{6,2},{0,4},{2,6},{5,1},{7,3},{1,5},{3,7},{12,8},{14,10},{8,... | collective-permute-start | bytes 1179656 | tf_op jit(solution)/shard_map/ppermute | solution.py:222
  88.0 21.2 %copy-start.5 = (bf16[1,1536,128]{2,1,0:T(8,128)(2,1)}, bf16[1,1536,128]{2,1,0:T(8,128)(2,1)S(1)}, u32[]{:S(2)}) copy-start(bf16[1,1536,128]{2,1,0:T(8,128)(2,1)S(1)} %collective-permute-done.11.refs_7_) | copy-start | bytes 1179652
  88.0 15.2 %collective-permute-start.12 = (bf16[1,1536,128]{2,1,0:T(8,128)(2,1)S(1)}, bf16[1,1536,128]{2,1,0:T(8,128)(2,1)S(1)}, u32[]{:S(2)}, u32[]{:S(2)}) collective-permute-start(bf16[1,1536,128]{2,1,0:T(8,128)(2,1)S(1)} %slice.16), channel_id=1, source_target_pairs={{2,0},{4,2},{6,4},{0,6},{3,1},{5,3},{7,5},{1,7},{10,8},{12,10},{14... | collective-permute-start | bytes 1179656 | tf_op jit(solution)/shard_map/ppermute | solution.py:222
  94.8 14.5 %copy-start.6 = (bf16[1,1536,128]{2,1,0:T(8,128)(2,1)}, bf16[1,1536,128]{2,1,0:T(8,128)(2,1)S(1)}, u32[]{:S(2)}) copy-start(bf16[1,1536,128]{2,1,0:T(8,128)(2,1)S(1)} %collective-permute-done.8.refs_4_) | copy-start | bytes 1179652
  94.8 14.4 %collective-permute-start.13 = (bf16[1,1536,128]{2,1,0:T(8,128)(2,1)S(1)}, bf16[1,1536,128]{2,1,0:T(8,128)(2,1)S(1)}, u32[]{:S(2)}, u32[]{:S(2)}) collective-permute-start(bf16[1,1536,128]{2,1,0:T(8,128)(2,1)S(1)} %slice.17), channel_id=1, source_target_pairs={{6,0},{0,2},{2,4},{4,6},{7,1},{1,3},{3,5},{5,7},{14,8},{8,10},{10,... | collective-permute-start | bytes 1179656 | tf_op jit(solution)/shard_map/ppermute | solution.py:222
  96.7 12.5 %copy-start.7 = (bf16[1,1536,128]{2,1,0:T(8,128)(2,1)}, bf16[1,1536,128]{2,1,0:T(8,128)(2,1)S(1)}, u32[]{:S(2)}) copy-start(bf16[1,1536,128]{2,1,0:T(8,128)(2,1)S(1)} %collective-permute-done.9.refs_5_) | copy-start | bytes 1179652
  102.5 6.7 %copy-start.8 = (bf16[1,1536,128]{2,1,0:T(8,128)(2,1)}, bf16[1,1536,128]{2,1,0:T(8,128)(2,1)S(1)}, u32[]{:S(2)}) copy-start(bf16[1,1536,128]{2,1,0:T(8,128)(2,1)S(1)} %collective-permute-done.10.refs_6_) | copy-start | bytes 1179652
  103.2 6.0 %copy-start.9 = (bf16[1,1536,128]{2,1,0:T(8,128)(2,1)}, bf16[1,1536,128]{2,1,0:T(8,128)(2,1)S(1)}, u32[]{:S(2)}) copy-start(bf16[1,1536,128]{2,1,0:T(8,128)(2,1)S(1)} %collective-permute-done.12.refs_8_) | copy-start | bytes 1179652
  109.3 0.8 copy-start.10
  115.1 64.3 %collective-permute-start.14 = (f32[256,1536]{1,0:T(8,128)S(1)}, f32[256,1536]{1,0:T(8,128)S(1)}, u32[]{:S(2)}, u32[]{:S(2)}) collective-permute-start(f32[256,1536]{1,0:T(8,128)S(1)} %get-tuple-element.11), channel_id=1, source_target_pairs={{1,0},{0,1},{3,2},{2,3},{5,4},{4,5},{7,6},{6,7},{9,8},{8,9},{11,10... | collective-permute-start | bytes 4718600 | tf_op jit(solution)/shard_map/ppermute | solution.py:293
  143.4 32.7 %collective-permute-start.1 = (bf16[8,264,128]{2,1,0:T(8,128)(2,1)S(1)}, bf16[8,264,128]{2,1,0:T(8,128)(2,1)S(1)}, u32[]{:S(2)}, u32[]{:S(2)}) collective-permute-start(bf16[8,264,128]{2,1,0:T(8,128)(2,1)S(1)} %all_to_all.20), channel_id=1, source_target_pairs={{256,0},{0,256},{257,1},{1,257},{258,2},{2,258},{259,3},{3,259},{2... | collective-permute-start | bytes 1622024 | tf_op jit(solution)/shard_map/ppermute | solution.py:273
  176.1 3.3 %copy-start = (bf16[1,1,256,3072]{3,2,1,0:T(8,128)(2,1)S(1)}, bf16[1,1,256,3072]{3,2,1,0:T(8,128)(2,1)}, u32[]{:S(2)}) copy-start(bf16[1,1,256,3072]{3,2,1,0:T(8,128)(2,1)} %param.8) | copy-start | bytes 4718596
  179.4 21.9 %copy-start.1 = (s32[128,8]{0,1:T(8,128)S(1)}, s32[128,8]{0,1:T(8,128)}, u32[]{:S(2)}) copy-start(s32[128,8]{0,1:T(8,128)} %param.6) | copy-start | bytes 12292
